TPU v7x, 32 devices: a whole 2x2x4 slice. The times are simulated.
32 devices in a mesh: gx: 4 (over x, core), gy: 2 (over y), gz: 4 (over z).
Axes of the slice: x: 2, y: 2, z: 4, core: 2. Of those that a mesh axis runs over, the one named last changes fastest.
Arguments:
- solution: float32 [16, 8, 16, 256], P(None, 'gx', 'gz', 'gy'), may hold values from -0.6 to 0.6
- residual: float32 [16, 8, 16, 256], P(None, 'gx', 'gz', 'gy'), may hold values from -6 to 6
- direction_prev: float32 [16, 8, 16, 256], P(None, 'gx', 'gz', 'gy'), may hold values from -0.3 to 0.3, as said below
- image_prev: float32 [16, 8, 16, 256], P(None, 'gx', 'gz', 'gy'), may hold values from -9 to 9, as said below
- gram_prev: float32 [16, 16], replicated, may hold values from -32768 to 32768, as said below
Outputs:
- solution_new: float32 [16, 8, 16, 256], P(None, 'gx', 'gz', 'gy')
- residual_new: float32 [16, 8, 16, 256], P(None, 'gx', 'gz', 'gy')
- direction: float32 [16, 8, 16, 256], P(None, 'gx', 'gz', 'gy')
Inputs may be any that keep to these rules, and one draw needn't show every extreme that they name: direction_prev is a field of order 0.05. image_prev equals A direction_prev, computed in float32. gram_prev is symmetric and positive definite.
All inputs are finite; a program needn't handle non-finite values.
Results may differ from a plain program's by a relative error of at most 0.0001.
Values sent between devices are 32-bit elements; how exact they have to be, the bound alone decides.
No kernel may reach another device: no remote copies, remote signals or barrier semaphores. Data moves between devices by JAX's collectives and lax.ppermute only.
A program may use at most 64 MiB of HBM per device.

v0:
```python
import jax
import jax.numpy as jnp
from jax import lax
from jax.sharding import PartitionSpec as P


def with_halo(value, sides, width):
    for axis, dim in sides:
        devices, length = (lax.axis_size(axis), value.shape[dim])
        up = [(i, (i + 1) % devices) for i in range(devices - 1)]
        down = [(j, i) for i, j in up]
        last = lax.slice_in_dim(value, length - width, length, axis=dim)
        first = lax.slice_in_dim(value, 0, width, axis=dim)
        before = lax.ppermute(last, axis, up)
        after = lax.ppermute(first, axis, down)
        value = jnp.concatenate([before, value, after], axis=dim)
    return value


def box_sum(padded):
    total = padded[:, :-2] + padded[:, 1:-1] + padded[:, 2:]
    total = total[:, :, :-2] + total[:, :, 1:-1] + total[:, :, 2:]
    return total[:, :, :, :-2] + total[:, :, :, 1:-1] + total[:, :, :, 2:]


def colors_of(shape):
    first = lax.broadcasted_iota(jnp.int32, shape, 1) % 2
    second = lax.broadcasted_iota(jnp.int32, shape, 2) % 2
    third = lax.broadcasted_iota(jnp.int32, shape, 3) % 2
    return 4 * first + 2 * second + third


def local_gram(left, right):
    return jnp.einsum("kxzy,lxzy->kl", left, right, precision=lax.Precision.HIGHEST)


def combine(field, mixing):
    return jnp.einsum("kxzy,kl->lxzy", field, mixing, precision=lax.Precision.HIGHEST)


def small_dot(left, right):
    return jnp.dot(left, right, precision=lax.Precision.HIGHEST)


def spd_solve(matrix, target):
    order = matrix.shape[0]
    sym = 0.5 * (matrix + matrix.T)
    lower = jnp.zeros_like(sym)
    for col in range(order):
        column = sym[col:, col] - jnp.sum(lower[col:, :col] * lower[col, :col][None, :], axis=1)
        pivot = jnp.sqrt(column[0])
        lower = lower.at[col:, col].set(column / pivot)
    middle = jnp.zeros_like(target)
    for row in range(order):
        value = target[row] - jnp.sum(lower[row, :row][:, None] * middle[:row], axis=0)
        middle = middle.at[row].set(value / lower[row, row])
    answer = jnp.zeros_like(target)
    for row in range(order - 1, -1, -1):
        value = middle[row] - jnp.sum(lower[row + 1 :, row][:, None] * answer[row + 1 :], axis=0)
        answer = answer.at[row].set(value / lower[row, row])
    return answer


def sweep_box(field):
    padded = with_halo(field, (("gx", 1), ("gy", 3), ("gz", 2)), 1)
    return box_sum(padded)


def body(solution, residual, direction_prev, image_prev, gram_prev):
    colors = colors_of(residual.shape)
    smoothed = jnp.where(colors == 0, residual / 26.0, jnp.float32(0.0))
    for shade in list(range(1, 8)) + list(range(6, -1, -1)):
        boxed = sweep_box(smoothed)
        smoothed = jnp.where(colors == shade, (residual + boxed - smoothed) / 26.0, smoothed)
    padded = with_halo(smoothed, (("gx", 1), ("gy", 3), ("gz", 2)), 1)
    image = 27.0 * smoothed - box_sum(padded)
    sums = (
        local_gram(smoothed, residual),
        local_gram(smoothed, image),
        local_gram(smoothed, image_prev),
        local_gram(direction_prev, image),
        local_gram(direction_prev, image_prev),
    )
    gram_zr, gram_zw, gram_zq, gram_pw, gram_pq = lax.psum(
        (sums[0], sums[1], sums[2], sums[3], sums[4]), ("gx", "gy", "gz")
    )
    beta_mix = spd_solve(gram_prev, gram_zr)
    direction = smoothed + combine(direction_prev, beta_mix)
    image_new = image + combine(image_prev, beta_mix)
    curvature = gram_zw + small_dot(gram_zq, beta_mix) + small_dot(beta_mix.T, gram_pw)
    curvature = curvature + small_dot(small_dot(beta_mix.T, gram_pq), beta_mix)
    alpha_step = spd_solve(curvature, gram_zr)
    solution_new = solution + combine(direction, alpha_step)
    residual_new = residual - combine(image_new, alpha_step)
    return (solution_new, residual_new, direction)


def solution(mesh):
    in_specs = (
        P(None, "gx", "gz", "gy"),
        P(None, "gx", "gz", "gy"),
        P(None, "gx", "gz", "gy"),
        P(None, "gx", "gz", "gy"),
        P(),
    )
    out_specs = (P(None, "gx", "gz", "gy"), P(None, "gx", "gz", "gy"), P(None, "gx", "gz", "gy"))
    return jax.shard_map(body, mesh=mesh, in_specs=in_specs, out_specs=out_specs, check_vma=False)
```

profile of v0, /device:TPU:0, one launch (start us, length us, event | category | flops | bytes accessed | tf_op | source)
XLA Modules:
  0.0 495.2 jit_solution(12396959425501181571)
XLA Ops:
  21.4 4.9 collective-permute-start.2
  30.6 6.1 %collective-permute-start.4 = (f32[16,4,1,130]{3,0,2,1:T(8,128)S(1)}, f32[16,4,1,130]{3,0,2,1:T(8,128)S(1)}, u32[]{:S(2)}, u32[]{:S(2)}) collective-permute-start(f32[16,4,1,130]{3,0,2,1:T(8,128)S(1)} %get-tuple-element.1202), channel_id=1, source_target_pairs={{0,1},{1,2},{2,3},{4,5},{5,6},{6,7},{8,9},{9,10},{10,11},{12,13},{... | collective-permute-start | bytes 99848 | tf_op jit(solution)/shard_map/ppermute | solution.py:14
  46.4 4.6 collective-permute-start.8
  55.6 4.8 collective-permute-start.10
  69.3 4.6 collective-permute-start.14
  78.5 4.9 collective-permute-start.16
  92.6 4.6 collective-permute-start.20
  101.1 5.0 %collective-permute-start.22 = (f32[16,4,1,130]{3,0,2,1:T(8,128)S(1)}, f32[16,4,1,130]{3,0,2,1:T(8,128)S(1)}, u32[]{:S(2)}, u32[]{:S(2)}) collective-permute-start(f32[16,4,1,130]{3,0,2,1:T(8,128)S(1)} %get-tuple-element.1196), channel_id=1, source_target_pairs={{0,1},{1,2},{2,3},{4,5},{5,6},{6,7},{8,9},{9,10},{10,11},{12,13},{... | collective-permute-start | bytes 99848 | tf_op jit(solution)/shard_map/ppermute | solution.py:14
  115.2 4.6 collective-permute-start.26
  123.7 5.0 %collective-permute-start.28 = (f32[16,4,1,130]{3,0,2,1:T(8,128)S(1)}, f32[16,4,1,130]{3,0,2,1:T(8,128)S(1)}, u32[]{:S(2)}, u32[]{:S(2)}) collective-permute-start(f32[16,4,1,130]{3,0,2,1:T(8,128)S(1)} %get-tuple-element.1194), channel_id=1, source_target_pairs={{0,1},{1,2},{2,3},{4,5},{5,6},{6,7},{8,9},{9,10},{10,11},{12,13},{... | collective-permute-start | bytes 99848 | tf_op jit(solution)/shard_map/ppermute | solution.py:14
  132.2 4.9 collective-permute-start.30
  147.9 4.6 collective-permute-start.34
  156.0 5.3 %collective-permute-start.36 = (f32[16,1,4,128]{3,0,2,1:T(8,128)S(1)}, f32[16,1,4,128]{3,0,2,1:T(8,128)S(1)}, u32[]{:S(2)}, u32[]{:S(2)}) collective-permute-start(f32[16,1,4,128]{3,0,2,1:T(8,128)S(1)} %get-tuple-element.1250), channel_id=1, source_target_pairs={{0,8},{8,16},{16,24},{1,9},{9,17},{17,25},{2,10},{10,18},{18,26},{... | collective-permute-start | bytes 98312 | tf_op jit(solution)/shard_map/ppermute | solution.py:14
  172.1 4.6 collective-permute-start.40
  180.3 5.3 %collective-permute-start.42 = (f32[16,1,4,128]{3,0,2,1:T(8,128)S(1)}, f32[16,1,4,128]{3,0,2,1:T(8,128)S(1)}, u32[]{:S(2)}, u32[]{:S(2)}) collective-permute-start(f32[16,1,4,128]{3,0,2,1:T(8,128)S(1)} %get-tuple-element.1248), channel_id=1, source_target_pairs={{0,8},{8,16},{16,24},{1,9},{9,17},{17,25},{2,10},{10,18},{18,26},{... | collective-permute-start | bytes 98312 | tf_op jit(solution)/shard_map/ppermute | solution.py:14
  196.3 4.8 collective-permute-start.46
  204.5 5.3 %collective-permute-start.48 = (f32[16,1,4,128]{3,0,2,1:T(8,128)S(1)}, f32[16,1,4,128]{3,0,2,1:T(8,128)S(1)}, u32[]{:S(2)}, u32[]{:S(2)}) collective-permute-start(f32[16,1,4,128]{3,0,2,1:T(8,128)S(1)} %get-tuple-element.1246), channel_id=1, source_target_pairs={{0,8},{8,16},{16,24},{1,9},{9,17},{17,25},{2,10},{10,18},{18,26},{... | collective-permute-start | bytes 98312 | tf_op jit(solution)/shard_map/ppermute | solution.py:14
  220.5 4.6 collective-permute-start.52
  228.7 5.3 %collective-permute-start.54 = (f32[16,1,4,128]{3,0,2,1:T(8,128)S(1)}, f32[16,1,4,128]{3,0,2,1:T(8,128)S(1)}, u32[]{:S(2)}, u32[]{:S(2)}) collective-permute-start(f32[16,1,4,128]{3,0,2,1:T(8,128)S(1)} %get-tuple-element.1244), channel_id=1, source_target_pairs={{0,8},{8,16},{16,24},{1,9},{9,17},{17,25},{2,10},{10,18},{18,26},{... | collective-permute-start | bytes 98312 | tf_op jit(solution)/shard_map/ppermute | solution.py:14
  244.8 4.6 collective-permute-start.58
  253.0 5.3 %collective-permute-start.60 = (f32[16,1,4,128]{3,0,2,1:T(8,128)S(1)}, f32[16,1,4,128]{3,0,2,1:T(8,128)S(1)}, u32[]{:S(2)}, u32[]{:S(2)}) collective-permute-start(f32[16,1,4,128]{3,0,2,1:T(8,128)S(1)} %get-tuple-element.1242), channel_id=1, source_target_pairs={{0,8},{8,16},{16,24},{1,9},{9,17},{17,25},{2,10},{10,18},{18,26},{... | collective-permute-start | bytes 98312 | tf_op jit(solution)/shard_map/ppermute | solution.py:14
  260.5 4.6 collective-permute-start.62
  269.0 4.6 collective-permute-start.64
  277.2 5.3 %collective-permute-start.66 = (f32[16,1,4,128]{3,0,2,1:T(8,128)S(1)}, f32[16,1,4,128]{3,0,2,1:T(8,128)S(1)}, u32[]{:S(2)}, u32[]{:S(2)}) collective-permute-start(f32[16,1,4,128]{3,0,2,1:T(8,128)S(1)} %get-tuple-element.1240), channel_id=1, source_target_pairs={{0,8},{8,16},{16,24},{1,9},{9,17},{17,25},{2,10},{10,18},{18,26},{... | collective-permute-start | bytes 98312 | tf_op jit(solution)/shard_map/ppermute | solution.py:14
  293.2 4.6 collective-permute-start.70
  301.4 5.3 %collective-permute-start.72 = (f32[16,1,4,128]{3,0,2,1:T(8,128)S(1)}, f32[16,1,4,128]{3,0,2,1:T(8,128)S(1)}, u32[]{:S(2)}, u32[]{:S(2)}) collective-permute-start(f32[16,1,4,128]{3,0,2,1:T(8,128)S(1)} %get-tuple-element.1238), channel_id=1, source_target_pairs={{0,8},{8,16},{16,24},{1,9},{9,17},{17,25},{2,10},{10,18},{18,26},{... | collective-permute-start | bytes 98312 | tf_op jit(solution)/shard_map/ppermute | solution.py:14
  317.5 4.6 collective-permute-start.76
  325.6 5.3 %collective-permute-start.78 = (f32[16,1,4,128]{3,0,2,1:T(8,128)S(1)}, f32[16,1,4,128]{3,0,2,1:T(8,128)S(1)}, u32[]{:S(2)}, u32[]{:S(2)}) collective-permute-start(f32[16,1,4,128]{3,0,2,1:T(8,128)S(1)} %get-tuple-element.1236), channel_id=1, source_target_pairs={{0,8},{8,16},{16,24},{1,9},{9,17},{17,25},{2,10},{10,18},{18,26},{... | collective-permute-start | bytes 98312 | tf_op jit(solution)/shard_map/ppermute | solution.py:14
  341.7 4.6 collective-permute-start.82
  349.9 5.3 %collective-permute-start.84 = (f32[16,1,4,128]{3,0,2,1:T(8,128)S(1)}, f32[16,1,4,128]{3,0,2,1:T(8,128)S(1)}, u32[]{:S(2)}, u32[]{:S(2)}) collective-permute-start(f32[16,1,4,128]{3,0,2,1:T(8,128)S(1)} %get-tuple-element.1234), channel_id=1, source_target_pairs={{0,8},{8,16},{16,24},{1,9},{9,17},{17,25},{2,10},{10,18},{18,26},{... | collective-permute-start | bytes 98312 | tf_op jit(solution)/shard_map/ppermute | solution.py:14
  367.0 4.6 collective-permute-start.88
  374.2 47.6 %all-reduce.6 = (f32[16,16]{1,0:T(8,128)S(1)}, f32[16,16]{1,0:T(8,128)S(1)}, f32[16,16]{1,0:T(8,128)S(1)}, f32[16,16]{0,1:T(8,128)S(1)}, f32[16,16]{1,0:T(8,128)S(1)}) all-reduce(f32[16,16]{1,0:T(8,128)S(1)} %convolution_bitcast_fusion.4, ...), channel_id=1, replica_groups=mesh['gx'=4,'gy'=2,'gz'=4] {'gx','gy','gz'}, use_global_device_ids=true, to_apply=%region_0.1 | all-reduce | flops 1280 | bytes 10240 | tf_op jit(solution)/shard_map/psum | solution.py:84
  (741 shorter events, 284.0 us)
Async XLA Ops:
  1.7 18.3 %collective-permute-start.1 = (f32[16,1,4,128]{3,0,2,1:T(8,128)S(1)}, f32[16,1,4,128]{3,0,2,1:T(8,128)S(1)}, u32[]{:S(2)}, u32[]{:S(2)}) collective-permute-start(f32[16,1,4,128]{3,0,2,1:T(8,128)S(1)} %get-tuple-element.1263), channel_id=1, source_target_pairs={{8,0},{16,8},{24,16},{9,1},{17,9},{25,17},{10,2},{18,10},{26,18},{... | collective-permute-start | bytes 98312 | tf_op jit(solution)/shard_map/ppermute | solution.py:15
  3.0 17.0 %collective-permute-start = (f32[16,1,4,128]{3,0,2,1:T(8,128)S(1)}, f32[16,1,4,128]{3,0,2,1:T(8,128)S(1)}, u32[]{:S(2)}, u32[]{:S(2)}) collective-permute-start(f32[16,1,4,128]{3,0,2,1:T(8,128)S(1)} %get-tuple-element.1262), channel_id=1, source_target_pairs={{0,8},{8,16},{16,24},{1,9},{9,17},{17,25},{2,10},{10,18},{18,26},{... | collective-permute-start | bytes 98312 | tf_op jit(solution)/shard_map/ppermute | solution.py:14
  20.1 7.4 %collective-permute-start.3 = (f32[16,4,4,1]{3,0,2,1:T(8,128)S(1)}, f32[16,4,4,1]{3,0,2,1:T(8,128)S(1)}, u32[]{:S(2)}, u32[]{:S(2)}) collective-permute-start(f32[16,4,4,1]{3,0,2,1:T(8,128)S(1)} %get-tuple-element.1233), channel_id=1, source_target_pairs={{4,0},{5,1},{6,2},{7,3},{12,8},{13,9},{14,10},{15,11},{20,16},{21,... | collective-permute-start | bytes 3080 | tf_op jit(solution)/shard_map/ppermute | solution.py:15
  21.4 7.8 %collective-permute-start.2 = (f32[16,4,4,1]{3,0,2,1:T(8,128)S(1)}, f32[16,4,4,1]{3,0,2,1:T(8,128)S(1)}, u32[]{:S(2)}, u32[]{:S(2)}) collective-permute-start(f32[16,4,4,1]{3,0,2,1:T(8,128)S(1)} %get-tuple-element.1232), channel_id=1, source_target_pairs={{0,4},{1,5},{2,6},{3,7},{8,12},{9,13},{10,14},{11,15},{16,20},{17,... | collective-permute-start | bytes 3080 | tf_op jit(solution)/shard_map/ppermute | solution.py:14
  29.3 7.8 %collective-permute-start.5 = (f32[16,4,1,130]{3,0,2,1:T(8,128)S(1)}, f32[16,4,1,130]{3,0,2,1:T(8,128)S(1)}, u32[]{:S(2)}, u32[]{:S(2)}) collective-permute-start(f32[16,4,1,130]{3,0,2,1:T(8,128)S(1)} %get-tuple-element.1203), channel_id=1, source_target_pairs={{1,0},{2,1},{3,2},{5,4},{6,5},{7,6},{9,8},{10,9},{11,10},{13,12},{... | collective-permute-start | bytes 99848 | tf_op jit(solution)/shard_map/ppermute | solution.py:15
  30.6 8.0 %collective-permute-start.4 = (f32[16,4,1,130]{3,0,2,1:T(8,128)S(1)}, f32[16,4,1,130]{3,0,2,1:T(8,128)S(1)}, u32[]{:S(2)}, u32[]{:S(2)}) collective-permute-start(f32[16,4,1,130]{3,0,2,1:T(8,128)S(1)} %get-tuple-element.1202), channel_id=1, source_target_pairs={{0,1},{1,2},{2,3},{4,5},{5,6},{6,7},{8,9},{9,10},{10,11},{12,13},{... | collective-permute-start | bytes 99848 | tf_op jit(solution)/shard_map/ppermute | solution.py:14
  45.1 7.9 %collective-permute-start.9 = (f32[16,4,4,1]{3,0,2,1:T(8,128)S(1)}, f32[16,4,4,1]{3,0,2,1:T(8,128)S(1)}, u32[]{:S(2)}, u32[]{:S(2)}) collective-permute-start(f32[16,4,4,1]{3,0,2,1:T(8,128)S(1)} %get-tuple-element.1231), channel_id=1, source_target_pairs={{4,0},{5,1},{6,2},{7,3},{12,8},{13,9},{14,10},{15,11},{20,16},{21,... | collective-permute-start | bytes 3080 | tf_op jit(solution)/shard_map/ppermute | solution.py:15
  46.4 7.8 %collective-permute-start.8 = (f32[16,4,4,1]{3,0,2,1:T(8,128)S(1)}, f32[16,4,4,1]{3,0,2,1:T(8,128)S(1)}, u32[]{:S(2)}, u32[]{:S(2)}) collective-permute-start(f32[16,4,4,1]{3,0,2,1:T(8,128)S(1)} %get-tuple-element.1230), channel_id=1, source_target_pairs={{0,4},{1,5},{2,6},{3,7},{8,12},{9,13},{10,14},{11,15},{16,20},{17,... | collective-permute-start | bytes 3080 | tf_op jit(solution)/shard_map/ppermute | solution.py:14
  68.0 7.4 %collective-permute-start.15 = (f32[16,4,4,1]{3,0,2,1:T(8,128)S(1)}, f32[16,4,4,1]{3,0,2,1:T(8,128)S(1)}, u32[]{:S(2)}, u32[]{:S(2)}) collective-permute-start(f32[16,4,4,1]{3,0,2,1:T(8,128)S(1)} %get-tuple-element.1229), channel_id=1, source_target_pairs={{4,0},{5,1},{6,2},{7,3},{12,8},{13,9},{14,10},{15,11},{20,16},{21,... | collective-permute-start | bytes 3080 | tf_op jit(solution)/shard_map/ppermute | solution.py:15
  69.3 7.8 %collective-permute-start.14 = (f32[16,4,4,1]{3,0,2,1:T(8,128)S(1)}, f32[16,4,4,1]{3,0,2,1:T(8,128)S(1)}, u32[]{:S(2)}, u32[]{:S(2)}) collective-permute-start(f32[16,4,4,1]{3,0,2,1:T(8,128)S(1)} %get-tuple-element.1228), channel_id=1, source_target_pairs={{0,4},{1,5},{2,6},{3,7},{8,12},{9,13},{10,14},{11,15},{16,20},{17,... | collective-permute-start | bytes 3080 | tf_op jit(solution)/shard_map/ppermute | solution.py:14
  77.2 7.2 %collective-permute-start.17 = (f32[16,4,1,130]{3,0,2,1:T(8,128)S(1)}, f32[16,4,1,130]{3,0,2,1:T(8,128)S(1)}, u32[]{:S(2)}, u32[]{:S(2)}) collective-permute-start(f32[16,4,1,130]{3,0,2,1:T(8,128)S(1)} %get-tuple-element.1199), channel_id=1, source_target_pairs={{1,0},{2,1},{3,2},{5,4},{6,5},{7,6},{9,8},{10,9},{11,10},{13,12},{... | collective-permute-start | bytes 99848 | tf_op jit(solution)/shard_map/ppermute | solution.py:15
  78.5 7.1 %collective-permute-start.16 = (f32[16,4,1,130]{3,0,2,1:T(8,128)S(1)}, f32[16,4,1,130]{3,0,2,1:T(8,128)S(1)}, u32[]{:S(2)}, u32[]{:S(2)}) collective-permute-start(f32[16,4,1,130]{3,0,2,1:T(8,128)S(1)} %get-tuple-element.1198), channel_id=1, source_target_pairs={{0,1},{1,2},{2,3},{4,5},{5,6},{6,7},{8,9},{9,10},{10,11},{12,13},{... | collective-permute-start | bytes 99848 | tf_op jit(solution)/shard_map/ppermute | solution.py:14
  91.3 6.9 %collective-permute-start.21 = (f32[16,4,4,1]{3,0,2,1:T(8,128)S(1)}, f32[16,4,4,1]{3,0,2,1:T(8,128)S(1)}, u32[]{:S(2)}, u32[]{:S(2)}) collective-permute-start(f32[16,4,4,1]{3,0,2,1:T(8,128)S(1)} %get-tuple-element.1227), channel_id=1, source_target_pairs={{4,0},{5,1},{6,2},{7,3},{12,8},{13,9},{14,10},{15,11},{20,16},{21,... | collective-permute-start | bytes 3080 | tf_op jit(solution)/shard_map/ppermute | solution.py:15
  92.6 7.1 %collective-permute-start.20 = (f32[16,4,4,1]{3,0,2,1:T(8,128)S(1)}, f32[16,4,4,1]{3,0,2,1:T(8,128)S(1)}, u32[]{:S(2)}, u32[]{:S(2)}) collective-permute-start(f32[16,4,4,1]{3,0,2,1:T(8,128)S(1)} %get-tuple-element.1226), channel_id=1, source_target_pairs={{0,4},{1,5},{2,6},{3,7},{8,12},{9,13},{10,14},{11,15},{16,20},{17,... | collective-permute-start | bytes 3080 | tf_op jit(solution)/shard_map/ppermute | solution.py:14
  101.1 7.0 %collective-permute-start.22 = (f32[16,4,1,130]{3,0,2,1:T(8,128)S(1)}, f32[16,4,1,130]{3,0,2,1:T(8,128)S(1)}, u32[]{:S(2)}, u32[]{:S(2)}) collective-permute-start(f32[16,4,1,130]{3,0,2,1:T(8,128)S(1)} %get-tuple-element.1196), channel_id=1, source_target_pairs={{0,1},{1,2},{2,3},{4,5},{5,6},{6,7},{8,9},{9,10},{10,11},{12,13},{... | collective-permute-start | bytes 99848 | tf_op jit(solution)/shard_map/ppermute | solution.py:14
  113.9 6.9 %collective-permute-start.27 = (f32[16,4,4,1]{3,0,2,1:T(8,128)S(1)}, f32[16,4,4,1]{3,0,2,1:T(8,128)S(1)}, u32[]{:S(2)}, u32[]{:S(2)}) collective-permute-start(f32[16,4,4,1]{3,0,2,1:T(8,128)S(1)} %get-tuple-element.1225), channel_id=1, source_target_pairs={{4,0},{5,1},{6,2},{7,3},{12,8},{13,9},{14,10},{15,11},{20,16},{21,... | collective-permute-start | bytes 3080 | tf_op jit(solution)/shard_map/ppermute | solution.py:15
  115.2 7.1 %collective-permute-start.26 = (f32[16,4,4,1]{3,0,2,1:T(8,128)S(1)}, f32[16,4,4,1]{3,0,2,1:T(8,128)S(1)}, u32[]{:S(2)}, u32[]{:S(2)}) collective-permute-start(f32[16,4,4,1]{3,0,2,1:T(8,128)S(1)} %get-tuple-element.1224), channel_id=1, source_target_pairs={{0,4},{1,5},{2,6},{3,7},{8,12},{9,13},{10,14},{11,15},{16,20},{17,... | collective-permute-start | bytes 3080 | tf_op jit(solution)/shard_map/ppermute | solution.py:14
  123.7 6.9 %collective-permute-start.28 = (f32[16,4,1,130]{3,0,2,1:T(8,128)S(1)}, f32[16,4,1,130]{3,0,2,1:T(8,128)S(1)}, u32[]{:S(2)}, u32[]{:S(2)}) collective-permute-start(f32[16,4,1,130]{3,0,2,1:T(8,128)S(1)} %get-tuple-element.1194), channel_id=1, source_target_pairs={{0,1},{1,2},{2,3},{4,5},{5,6},{6,7},{8,9},{9,10},{10,11},{12,13},{... | collective-permute-start | bytes 99848 | tf_op jit(solution)/shard_map/ppermute | solution.py:14
  138.1 6.9 %collective-permute-start.33 = (f32[16,4,4,1]{3,0,2,1:T(8,128)S(1)}, f32[16,4,4,1]{3,0,2,1:T(8,128)S(1)}, u32[]{:S(2)}, u32[]{:S(2)}) collective-permute-start(f32[16,4,4,1]{3,0,2,1:T(8,128)S(1)} %get-tuple-element.1223), channel_id=1, source_target_pairs={{4,0},{5,1},{6,2},{7,3},{12,8},{13,9},{14,10},{15,11},{20,16},{21,... | collective-permute-start | bytes 3080 | tf_op jit(solution)/shard_map/ppermute | solution.py:15
  139.4 7.1 %collective-permute-start.32 = (f32[16,4,4,1]{3,0,2,1:T(8,128)S(1)}, f32[16,4,4,1]{3,0,2,1:T(8,128)S(1)}, u32[]{:S(2)}, u32[]{:S(2)}) collective-permute-start(f32[16,4,4,1]{3,0,2,1:T(8,128)S(1)} %get-tuple-element.1222), channel_id=1, source_target_pairs={{0,4},{1,5},{2,6},{3,7},{8,12},{9,13},{10,14},{11,15},{16,20},{17,... | collective-permute-start | bytes 3080 | tf_op jit(solution)/shard_map/ppermute | solution.py:14
  163.6 7.1 %collective-permute-start.38 = (f32[16,4,4,1]{3,0,2,1:T(8,128)S(1)}, f32[16,4,4,1]{3,0,2,1:T(8,128)S(1)}, u32[]{:S(2)}, u32[]{:S(2)}) collective-permute-start(f32[16,4,4,1]{3,0,2,1:T(8,128)S(1)} %get-tuple-element.1220), channel_id=1, source_target_pairs={{0,4},{1,5},{2,6},{3,7},{8,12},{9,13},{10,14},{11,15},{16,20},{17,... | collective-permute-start | bytes 3080 | tf_op jit(solution)/shard_map/ppermute | solution.py:14
  187.8 7.1 %collective-permute-start.44 = (f32[16,4,4,1]{3,0,2,1:T(8,128)S(1)}, f32[16,4,4,1]{3,0,2,1:T(8,128)S(1)}, u32[]{:S(2)}, u32[]{:S(2)}) collective-permute-start(f32[16,4,4,1]{3,0,2,1:T(8,128)S(1)} %get-tuple-element.1218), channel_id=1, source_target_pairs={{0,4},{1,5},{2,6},{3,7},{8,12},{9,13},{10,14},{11,15},{16,20},{17,... | collective-permute-start | bytes 3080 | tf_op jit(solution)/shard_map/ppermute | solution.py:14
  212.1 7.1 %collective-permute-start.50 = (f32[16,4,4,1]{3,0,2,1:T(8,128)S(1)}, f32[16,4,4,1]{3,0,2,1:T(8,128)S(1)}, u32[]{:S(2)}, u32[]{:S(2)}) collective-permute-start(f32[16,4,4,1]{3,0,2,1:T(8,128)S(1)} %get-tuple-element.1216), channel_id=1, source_target_pairs={{0,4},{1,5},{2,6},{3,7},{8,12},{9,13},{10,14},{11,15},{16,20},{17,... | collective-permute-start | bytes 3080 | tf_op jit(solution)/shard_map/ppermute | solution.py:14
  227.4 7.3 %collective-permute-start.55 = (f32[16,1,4,128]{3,0,2,1:T(8,128)S(1)}, f32[16,1,4,128]{3,0,2,1:T(8,128)S(1)}, u32[]{:S(2)}, u32[]{:S(2)}) collective-permute-start(f32[16,1,4,128]{3,0,2,1:T(8,128)S(1)} %get-tuple-element.1245), channel_id=1, source_target_pairs={{8,0},{16,8},{24,16},{9,1},{17,9},{25,17},{10,2},{18,10},{26,18},{... | collective-permute-start | bytes 98312 | tf_op jit(solution)/shard_map/ppermute | solution.py:15
  236.3 7.1 %collective-permute-start.56 = (f32[16,4,4,1]{3,0,2,1:T(8,128)S(1)}, f32[16,4,4,1]{3,0,2,1:T(8,128)S(1)}, u32[]{:S(2)}, u32[]{:S(2)}) collective-permute-start(f32[16,4,4,1]{3,0,2,1:T(8,128)S(1)} %get-tuple-element.1214), channel_id=1, source_target_pairs={{0,4},{1,5},{2,6},{3,7},{8,12},{9,13},{10,14},{11,15},{16,20},{17,... | collective-permute-start | bytes 3080 | tf_op jit(solution)/shard_map/ppermute | solution.py:14
  260.5 7.1 %collective-permute-start.62 = (f32[16,4,4,1]{3,0,2,1:T(8,128)S(1)}, f32[16,4,4,1]{3,0,2,1:T(8,128)S(1)}, u32[]{:S(2)}, u32[]{:S(2)}) collective-permute-start(f32[16,4,4,1]{3,0,2,1:T(8,128)S(1)} %get-tuple-element.1212), channel_id=1, source_target_pairs={{0,4},{1,5},{2,6},{3,7},{8,12},{9,13},{10,14},{11,15},{16,20},{17,... | collective-permute-start | bytes 3080 | tf_op jit(solution)/shard_map/ppermute | solution.py:14
  284.8 7.1 %collective-permute-start.68 = (f32[16,4,4,1]{3,0,2,1:T(8,128)S(1)}, f32[16,4,4,1]{3,0,2,1:T(8,128)S(1)}, u32[]{:S(2)}, u32[]{:S(2)}) collective-permute-start(f32[16,4,4,1]{3,0,2,1:T(8,128)S(1)} %get-tuple-element.1210), channel_id=1, source_target_pairs={{0,4},{1,5},{2,6},{3,7},{8,12},{9,13},{10,14},{11,15},{16,20},{17,... | collective-permute-start | bytes 3080 | tf_op jit(solution)/shard_map/ppermute | solution.py:14
  309.0 7.1 %collective-permute-start.74 = (f32[16,4,4,1]{3,0,2,1:T(8,128)S(1)}, f32[16,4,4,1]{3,0,2,1:T(8,128)S(1)}, u32[]{:S(2)}, u32[]{:S(2)}) collective-permute-start(f32[16,4,4,1]{3,0,2,1:T(8,128)S(1)} %get-tuple-element.1208), channel_id=1, source_target_pairs={{0,4},{1,5},{2,6},{3,7},{8,12},{9,13},{10,14},{11,15},{16,20},{17,... | collective-permute-start | bytes 3080 | tf_op jit(solution)/shard_map/ppermute | solution.py:14
  333.2 7.1 %collective-permute-start.80 = (f32[16,4,4,1]{3,0,2,1:T(8,128)S(1)}, f32[16,4,4,1]{3,0,2,1:T(8,128)S(1)}, u32[]{:S(2)}, u32[]{:S(2)}) collective-permute-start(f32[16,4,4,1]{3,0,2,1:T(8,128)S(1)} %get-tuple-element.1206), channel_id=1, source_target_pairs={{0,4},{1,5},{2,6},{3,7},{8,12},{9,13},{10,14},{11,15},{16,20},{17,... | collective-permute-start | bytes 3080 | tf_op jit(solution)/shard_map/ppermute | solution.py:14
  348.6 8.4 %collective-permute-start.85 = (f32[16,1,4,128]{3,0,2,1:T(8,128)S(1)}, f32[16,1,4,128]{3,0,2,1:T(8,128)S(1)}, u32[]{:S(2)}, u32[]{:S(2)}) collective-permute-start(f32[16,1,4,128]{3,0,2,1:T(8,128)S(1)} %get-tuple-element.1235), channel_id=1, source_target_pairs={{8,0},{16,8},{24,16},{9,1},{17,9},{25,17},{10,2},{18,10},{26,18},{... | collective-permute-start | bytes 98312 | tf_op jit(solution)/shard_map/ppermute | solution.py:15
  349.9 7.2 %collective-permute-start.84 = (f32[16,1,4,128]{3,0,2,1:T(8,128)S(1)}, f32[16,1,4,128]{3,0,2,1:T(8,128)S(1)}, u32[]{:S(2)}, u32[]{:S(2)}) collective-permute-start(f32[16,1,4,128]{3,0,2,1:T(8,128)S(1)} %get-tuple-element.1234), channel_id=1, source_target_pairs={{0,8},{8,16},{16,24},{1,9},{9,17},{17,25},{2,10},{10,18},{18,26},{... | collective-permute-start | bytes 98312 | tf_op jit(solution)/shard_map/ppermute | solution.py:14
  358.5 7.1 %collective-permute-start.86 = (f32[16,4,4,1]{3,0,2,1:T(8,128)S(1)}, f32[16,4,4,1]{3,0,2,1:T(8,128)S(1)}, u32[]{:S(2)}, u32[]{:S(2)}) collective-permute-start(f32[16,4,4,1]{3,0,2,1:T(8,128)S(1)} %get-tuple-element.1204), channel_id=1, source_target_pairs={{0,4},{1,5},{2,6},{3,7},{8,12},{9,13},{10,14},{11,15},{16,20},{17,... | collective-permute-start | bytes 3080 | tf_op jit(solution)/shard_map/ppermute | solution.py:14
  (63 other events, 596.6 us)
where the time goes:
time: 498 us; the launch traced here: 495 us
  starting transfers between devices  267 us (54%)
  waiting for transfers between devices  71.8 us (14%)
  other arithmetic  62.7 us (13%)
  blocking collectives  47.6 us (10%)
  local copies, waits for them, and re-layouts  32.4 us (7%)
  between operations  11.3 us (2%)
    ppermute x45, starting transfers between devices, with_halo(): before = lax.ppermute(last, axis, up)  209 us
    ppermute x45, starting transfers between devices, with_halo(): after = lax.ppermute(first, axis, down)  58.1 us
    ppermute x45, waiting for transfers between devices, with_halo(): before = lax.ppermute(last, axis, up)  54.6 us
    psum x1, blocking collectives, body(): lax.psum((sums[0], sums[1], sums[2], sums[3], sums[4]), ('gx', 'gy', 'gz'))  47.6 us
    div x30, other arithmetic, spd_solve(): answer = answer.at[row].set(value / lower[row, row])  20.1 us
    div x28, other arithmetic, spd_solve(): middle = middle.at[row].set(value / lower[row, row])  20.1 us
    ppermute x45, waiting for transfers between devices, with_halo(): after = lax.ppermute(first, axis, down)  17.2 us
  transfers between devices with their start and end apart: 90, of which 71 were waited for; matrix products, arithmetic and copies ran while one was open for 4% of the time, Pallas kernels for 0%

commit v1 on v0

v1 whole, which is shorter than its diff:
```python
import functools

import jax
import jax.numpy as jnp
from jax import lax
from jax.experimental import pallas as pl
from jax.experimental.pallas import tpu as pltpu
from jax.sharding import PartitionSpec as P

HIGHEST = lax.Precision.HIGHEST
REACH = {"gx": (2, 3), "gz": (6, 7), "gy": (14, 15)}
HALO = 16


def shifted(value, axis, step):
    devices = lax.axis_size(axis)
    pairs = [(i, i - step) for i in range(devices) if 0 <= i - step < devices]
    return lax.ppermute(value, axis, pairs)


def block_reach(axis, length):
    low, high = REACH[axis]
    return (-(-low // length), -(-high // length))


def gathered(axis, length):
    low, high = block_reach(axis, length)
    return lax.axis_size(axis) <= low + high + 1


def neighbours(value, axis, length):
    if gathered(axis, length):
        return lax.all_gather(value, axis)
    low, high = block_reach(axis, length)
    return jnp.stack([value if s == 0 else shifted(value, axis, s) for s in range(-low, high + 1)])


def beside(value):
    devices, width = (lax.axis_size("gy"), HALO)
    first, last = value[..., :width], value[..., -width:]
    if devices == 2:
        both = lax.ppermute(jnp.concatenate([first, last], axis=-1), "gy", [(0, 1), (1, 0)])
    else:
        both = jnp.concatenate([shifted(first, "gy", 1), shifted(last, "gy", -1)], axis=-1)
    rows, rhs, lanes = value.shape
    group = lanes // (2 * width)
    both = both.reshape(rows // group, group, rhs, 2, width).transpose(0, 2, 3, 1, 4)
    return both.reshape(rows // group, rhs, lanes)


def smooth_kernel(where, upper, lower, prev, image_prev, smoothed_out, image_out, gram_out, x00, x01, x10, x11, *, dims, counts, full):
    lx, lz, rows, lanes = dims
    nx, nz, ny = counts
    at_x, at_z, at_y = where[0], where[1], where[2]
    total = 2 * lanes
    lane = lax.broadcasted_iota(jnp.int32, (1, total), 1)
    half = lanes // 2
    group = half // HALO
    inside = jnp.ones((1, total), jnp.float32)
    inside = jnp.where((lane >= lanes) & (lane < lanes + half) & (at_y == ny - 1), 0.0, inside)
    inside = jnp.where((lane >= lanes + half) & (at_y == 0), 0.0, inside)
    inside = inside * (1.0 / 26.0)
    even_lanes = jnp.where(lane % 2 == 0, inside, 0.0)
    odd_lanes = jnp.where(lane % 2 == 1, inside, 0.0)
    low_x, low_z = block_low("gx", lx), block_low("gz", lz)

    def source(li, lj):
        gi, gj = at_x * lx + li, at_z * lz + lj
        valid = (gi >= 0) & (gi < nx * lx) & (gj >= 0) & (gj < nz * lz)
        gi, gj = jnp.clip(gi, 0, nx * lx - 1), jnp.clip(gj, 0, nz * lz - 1)
        bx, bz = gi // lx, gj // lz
        sub = (gi - bx * lx) * lz + gj - bz * lz
        bx = bx if full[0] else bx - at_x + low_x
        bz = bz if full[1] else bz - at_z + low_z
        scale = jnp.where(valid, 1.0, 0.0).astype(jnp.float32)
        place = (lj % lz) % group
        main = jnp.concatenate([upper[bx, bz, sub], lower[bx, bz, sub]], axis=0)
        packed = rows + sub // group
        tile = jnp.concatenate([upper[bx, bz, packed], lower[bx, bz, packed]], axis=0)
        after = pltpu.roll(tile, (lanes - HALO * place) % lanes, 1)
        before = pltpu.roll(tile, (half - HALO * (place + 1)) % lanes, 1)
        side = jnp.where(lane[:, :lanes] < half, after, before)
        return jnp.concatenate([main, side], axis=1), even_lanes * scale, odd_lanes * scale

    def pair(x):
        return pltpu.roll(x, 1, 1) + pltpu.roll(x, total - 1, 1)

    def box(x):
        return x + pair(x)

    ex, ez = lx // 2 + 3, (lz + 14) // 2

    def sides_j0(ref, a, b):
        return ref[a, b - 1] + ref[a, b]

    def sides_j1(ref, a, b):
        return ref[a, b] + ref[a, b + 1]

    def loop(count, start, step):
        def run(a, carry):
            step(a)
            return carry

        lax.fori_loop(start, start + count, run, 0)

    def f0e(a):
        for b in range(ez):
            r, se, so = source(-2 + 2 * a, -6 + 2 * b)
            xe = r * se
            x00[a, b] = xe + (r + pair(xe)) * so

    def f0o(a):
        for b in range(ez - 1):
            r, se, so = source(-2 + 2 * a, -5 + 2 * b)
            q = r + box(sides_j1(x00, a, b))
            xe = q * se
            x01[a, b] = xe + (q + pair(xe)) * so

    def f1e(a):
        for b in range(1, ez - 1):
            r, se, so = source(-1 + 2 * a, -6 + 2 * b)
            near = x00[a, b] + x00[a + 1, b] + sides_j0(x01, a, b) + sides_j0(x01, a + 1, b)
            q = r + box(near)
            xe = q * se
            x10[a, b] = xe + (q + pair(xe)) * so

    def f1o(a):
        for b in range(1, ez - 2):
            r, se, so = source(-1 + 2 * a, -5 + 2 * b)
            near = x01[a, b] + x01[a + 1, b] + sides_j1(x00, a, b) + sides_j1(x00, a + 1, b) + sides_j1(x10, a, b)
            q = r + box(near)
            xo = (q + pair(q * se)) * so
            x11[a, b] = (q + pair(xo)) * se + xo

    def b1e(a):
        for b in range(2, ez - 2):
            r, se, so = source(-1 + 2 * a, -6 + 2 * b)
            near = x00[a, b] + x00[a + 1, b] + sides_j0(x01, a, b) + sides_j0(x01, a + 1, b) + sides_j0(x11, a, b)
            q = r + box(near)
            xo = (q + pair(x10[a, b])) * so
            x10[a, b] = (q + pair(xo)) * se + xo

    def b0o(a):
        for b in range(2, ez - 3):
            r, se, so = source(-2 + 2 * a, -5 + 2 * b)
            near = x11[a - 1, b] + x11[a, b] + sides_j1(x10, a - 1, b) + sides_j1(x10, a, b) + sides_j1(x00, a, b)
            q = r + box(near)
            xo = (q + pair(x01[a, b])) * so
            x01[a, b] = (q + pair(xo)) * se + xo

    def b0e(a):
        for b in range(3, ez - 3):
            r, se, so = source(-2 + 2 * a, -6 + 2 * b)
            near = x10[a - 1, b] + x10[a, b] + sides_j0(x11, a - 1, b) + sides_j0(x11, a, b) + sides_j0(x01, a, b)
            q = r + box(near)
            xo = (q + pair(x00[a, b])) * so
            x00[a, b] = (q + pair(xo)) * se + xo

    loop(ex, 0, f0e)
    loop(ex, 0, f0o)
    loop(ex - 1, 0, f1e)
    loop(ex - 1, 0, f1o)
    loop(ex - 1, 0, b1e)
    loop(ex - 2, 1, b0o)
    loop(ex - 2, 1, b0e)

    def cell(i, j):
        a = (i + 2) // 2 if i % 2 == 0 else (i + 1) // 2
        b = (j + 6) // 2 if j % 2 == 0 else (j + 5) // 2
        return ((x00, x01), (x10, x11))[i % 2][j % 2][a, b]

    own = []
    for i in range(lx):
        for j in range(lz):
            near = functools.reduce(jnp.add, [cell(i + u, j + v) for u in (-1, 0, 1) for v in (-1, 0, 1)])
            mine = cell(i, j)
            image = 27.0 * mine - box(near)
            at = (i * lz + j) * lanes
            smoothed_out[:, at : at + lanes] = mine[:, :lanes]
            image_out[:, at : at + lanes] = image[:, :lanes]
            own.append(source(i, j)[0][:, :lanes])
    left = jnp.concatenate([smoothed_out[...], prev[...]], axis=0)
    right = jnp.concatenate([jnp.concatenate(own, axis=1), image_out[...], image_prev[...]], axis=0)
    gram_out[...] = lax.dot_general(left, right, (((1,), (1,)), ((), ())), precision=HIGHEST)


def block_low(axis, length):
    return -(-REACH[axis][0] // length)


def spd_solve(matrix, target):
    order = matrix.shape[0]
    sym = 0.5 * (matrix + matrix.T)
    work = jnp.concatenate([sym, target], axis=1)
    row = lax.broadcasted_iota(jnp.int32, (order, 1), 0)
    for k in range(order):
        scaled = work[k : k + 1] / work[k : k + 1, k : k + 1]
        factor = work[:, k : k + 1]
        work = jnp.where(row == k, scaled, work - factor * scaled)
    return work[:, order:]


def dot(left, right):
    return jnp.dot(left, right, precision=HIGHEST)


def finish_kernel(grams, gram_prev, solution, residual, prev, image_prev, smoothed, image, solution_out, residual_out, direction_out):
    n = gram_prev.shape[0]
    total = jnp.sum(grams[...], axis=0)
    gram_zr, gram_zw, gram_zq = total[:n, :n], total[:n, n : 2 * n], total[:n, 2 * n :]
    gram_pw, gram_pq = total[n:, n : 2 * n], total[n:, 2 * n :]
    beta = spd_solve(gram_prev[...], gram_zr)
    turned = beta.T
    curvature = gram_zw + dot(gram_zq, beta) + dot(turned, gram_pw + dot(gram_pq, beta))
    direction = smoothed[...] + dot(turned, prev[...])
    image_new = image[...] + dot(turned, image_prev[...])
    alpha = spd_solve(curvature, gram_zr).T
    direction_out[...] = direction
    solution_out[...] = solution[...] + dot(alpha, direction)
    residual_out[...] = residual[...] - dot(alpha, image_new)


def gather_grams(gram):
    for axis in ("gx", "gy", "gz"):
        others = [lax.ppermute(gram, axis, [(i, (i + k) % lax.axis_size(axis)) for i in range(lax.axis_size(axis))])
                  for k in range(1, lax.axis_size(axis))]
        gram = functools.reduce(jnp.add, others, gram)
    return gram[None]


def body(solution, residual, direction_prev, image_prev, gram_prev):
    rhs, lx, lz, lanes = residual.shape
    rows = lx * lz
    counts = tuple(lax.axis_size(axis) for axis in ("gx", "gz", "gy"))
    where = jnp.stack([lax.axis_index(axis) for axis in ("gx", "gz", "gy")]).astype(jnp.int32)
    flat = [v.reshape(rhs, rows * lanes) for v in (solution, residual, direction_prev, image_prev)]
    turned = residual.transpose(1, 2, 0, 3).reshape(rows, rhs, lanes)
    wide = jnp.concatenate([turned, beside(turned)], axis=0)
    wide = neighbours(wide, "gz", lz)
    upper = neighbours(wide[:, :, : rhs // 2], "gx", lx)
    lower = neighbours(wide[:, :, rhs // 2 :], "gx", lx)
    full = (gathered("gx", lx), gathered("gz", lz))
    ex, ez = lx // 2 + 3, (lz + 14) // 2
    out = jax.ShapeDtypeStruct((rhs, rows * lanes), jnp.float32)
    vmem = pl.BlockSpec(memory_space=pltpu.VMEM)
    smoothed, image, gram = pl.pallas_call(
        functools.partial(smooth_kernel, dims=(lx, lz, rows, lanes), counts=counts, full=full),
        out_shape=(out, out, jax.ShapeDtypeStruct((2 * rhs, 3 * rhs), jnp.float32)),
        in_specs=[pl.BlockSpec(memory_space=pltpu.SMEM)] + [vmem] * 4,
        out_specs=(vmem, vmem, vmem),
        scratch_shapes=[pltpu.VMEM((ex, ez, rhs, 2 * lanes), jnp.float32) for _ in range(4)],
        name="smooth",
    )(where, upper, lower, flat[2], flat[3])
    grams = gather_grams(gram)
    outs = pl.pallas_call(
        finish_kernel,
        out_shape=(out, out, out),
        in_specs=[vmem] * 8,
        out_specs=(vmem,) * 3,
        name="finish",
    )(grams, gram_prev, *flat, smoothed, image)
    return tuple(v.reshape(residual.shape) for v in outs)


def solution(mesh):
    field = P(None, "gx", "gz", "gy")
    return jax.shard_map(
        body, mesh=mesh, in_specs=(field,) * 4 + (P(),), out_specs=(field,) * 3, check_vma=False
    )
```

time: 498 us -> 74.2 us (0.15)
  starting transfers between devices: 267 us -> 10.8 us
  waiting for transfers between devices: 71.8 us -> 7.17 us
  other arithmetic: 62.7 us -> 2.08 us
  local copies, waits for them, and re-layouts: 32.4 us -> 7.14 us
  blocking collectives: 47.6 us -> 31.6 us
  Pallas kernels: 0 us -> 14.2 us
  between operations: 11.3 us -> 0.69 us
    ppermute x90 -> x8, starting transfers between devices: 267 us -> 10.8 us  [the longest x7 7.78 us: gather_grams(): lax.ppermute(gram, axis, [(i, (i + k) % lax.axis_size(axis)) for i in ran...]
    ppermute x90 -> x8, waiting for transfers between devices: 71.8 us -> 7.17 us  [the longest x7 7.07 us: gather_grams(): lax.ppermute(gram, axis, [(i, (i + k) % lax.axis_size(axis)) for i in ran...]
    psum x1 -> x0, blocking collectives: 47.6 us -> none  [body(): lax.psum((sums[0], sums[1], sums[2], sums[3], sums[4]), ('gx', 'gy', 'gz'))]
    div x86 -> x0, other arithmetic: 42.1 us -> none  [the longest x30 20.1 us: spd_solve(): answer = answer.at[row].set(value / lower[row, row])]
    all_gather x0 -> x3, blocking collectives: none -> 31.6 us  [neighbours(): return lax.all_gather(value, axis)]
    slice x94 -> x2, local copies, waits for them, and re-layouts: 16.9 us -> 0.1 us  [the longest x1 0.08 us: beside(): first, last = (value[..., :width], value[..., -width:])]
    pallas_call x0 -> x2, Pallas kernels: none -> 14.2 us  [the longest x1 8.55 us: body(): pl.pallas_call(functools.partial(smooth_kernel, dims=(lx, lz, rows, lanes...]
    scatter x92 -> x0, local copies, waits for them, and re-layouts: 9.63 us -> none  [the longest x30 7.29 us: spd_solve(): lower = lower.at[col:, col].set(column / pivot)]
  transfers between devices with their start and end apart: 90 -> 8, of which waited for: 71 -> 6; matrix products, arithmetic and copies ran while one was open for 4% -> 4% of each run, Pallas kernels for 0% -> 0%
where the time goes in v1:
time: 74.2 us; the launch traced here: 73.8 us
  blocking collectives  31.6 us (43%)
  Pallas kernels  14.2 us (19%)
  starting transfers between devices  10.8 us (15%)
  waiting for transfers between devices  7.17 us (10%)
  local copies, waits for them, and re-layouts  7.14 us (10%)
  other arithmetic  2.08 us (3%)
    all_gather x3, blocking collectives, neighbours(): return lax.all_gather(value, axis)  31.6 us
    pallas_call x1, Pallas kernels, body(): pl.pallas_call(functools.partial(smooth_kernel, dims=(lx, lz, rows, lanes...  8.55 us
    ppermute x7, starting transfers between devices, gather_grams(): lax.ppermute(gram, axis, [(i, (i + k) % lax.axis_size(axis)) for i in ran...  7.78 us
    ppermute x7, waiting for transfers between devices, gather_grams(): lax.ppermute(gram, axis, [(i, (i + k) % lax.axis_size(axis)) for i in ran...  7.07 us
    pallas_call x1, Pallas kernels, body(): pl.pallas_call(finish_kernel, out_shape=(out, out, out), in_specs=[vmem]...  5.7 us
    ppermute x1, starting transfers between devices, beside(): lax.ppermute(jnp.concatenate([first, last], axis=-1), 'gy', [(0, 1), (1,...  3.06 us
    reshape x3, local copies, waits for them, and re-layouts, body(): return tuple((v.reshape(residual.shape) for v in outs))  2.85 us
    reshape x4, local copies, waits for them, and re-layouts, body(): v.reshape(rhs, rows * lanes)  2.62 us
  transfers between devices with their start and end apart: 8, of which 6 were waited for; matrix products, arithmetic and copies ran while one was open for 4% of the time, Pallas kernels for 0%

profile of v1, /device:TPU:0, one launch (start us, length us, event | category | flops | bytes accessed | tf_op | source)
XLA Modules:
  0.0 73.8 jit_solution(16481092708785411900)
XLA Ops:
  0.6 0.9 %copy.10 = f32[2,4,16,128]{3,2,1,0:T(8,128)S(1)} copy(f32[2,4,16,128]{3,1,0,2:T(4,128)} %bitcast.19) | data formatting | bytes 131072 | tf_op jit(solution)/shard_map/transpose | solution.py:237
  1.7 3.1 %collective-permute-start = (f32[8,16,32]{2,1,0:T(8,128)S(1)}, f32[8,16,32]{2,1,0:T(8,128)S(1)}, u32[]{:S(2)}, u32[]{:S(2)}) collective-permute-start(f32[8,16,32]{2,1,0:T(8,128)S(1)} %pad_maximum_fusion.1), channel_id=1, source_target_pairs={{0,4},{4,0},{1,5},{5,1},{2,6},{6,2},{3,7},{7,3},{8,12},{12,8},{9,1... | collective-permute-start | bytes 49160 | tf_op jit(solution)/shard_map/ppermute | solution.py:42
  4.7 0.7 pad_add_fusion.where
  5.4 0.7 reshape.39.prev
  6.0 0.2 copy-done.2
  6.2 0.7 reshape.40.image_prev
  7.0 0.1 reshape.37
  7.2 0.1 reshape.38
  7.3 14.8 %all-gather = f32[40,16,128]{2,1,0:T(8,128)S(1)} all-gather(f32[10,16,128]{2,1,0:T(8,128)S(1)} %pad_maximum_fusion), channel_id=2, replica_groups=mesh['gx'=4,'gy'=2,'gz'=4] {'gz'}, dimensions={0}, use_global_device_ids=true | all-gather | bytes 409600 | tf_op jit(solution)/shard_map/all_gather | solution.py:33
  22.2 8.3 %all-gather.1 = f32[16,10,8,128]{3,2,1,0:T(8,128)} all-gather(f32[4,10,8,128]{3,2,1,0:T(8,128)S(1)} %get-tuple-element.16), channel_id=3, replica_groups=mesh['gx'=4,'gy'=2,'gz'=4] {'gx'}, dimensions={0}, use_global_device_ids=true | all-gather | bytes 819200 | tf_op jit(solution)/shard_map/all_gather | solution.py:33
  30.5 8.4 %all-gather.2 = f32[16,10,8,128]{3,2,1,0:T(8,128)} all-gather(f32[4,10,8,128]{3,2,1,0:T(8,128)S(1)} %get-tuple-element.15), channel_id=4, replica_groups=mesh['gx'=4,'gy'=2,'gz'=4] {'gx'}, dimensions={0}, use_global_device_ids=true | all-gather | bytes 819200 | tf_op jit(solution)/shard_map/all_gather | solution.py:33
  39.0 8.6 %smooth.1 = (f32[16,1024]{1,0:T(8,128)}, f32[16,1024]{1,0:T(8,128)}, f32[32,48]{1,0:T(8,128)}) custom-call(s32[3]{0:T(128)} %pad_add_fusion.where, f32[4,4,10,8,128]{4,3,2,1,0:T(8,128)} %bitcast.13, f32[4,4,10,8,128]{4,3,2,1,0:T(8,128)} %bitcast.14, f32[16,1024]{1,0:T(8,128)} %reshape.39.prev, f32[16,1024]{1,0:T(8,128)} %reshape.40.image_prev), custom_call_target="tpu_custom_call" | custom-call | tf_op jit(solution)/shard_map/smooth/pallas_call | solution.py:246
  47.5 0.4 collective-permute-start.1
  47.9 0.5 collective-permute-start.2
  48.4 1.1 %collective-permute-start.3 = (f32[32,48]{1,0:T(8,128)}, f32[32,48]{1,0:T(8,128)S(1)}, u32[]{:S(2)}, u32[]{:S(2)}) collective-permute-start(f32[32,48]{1,0:T(8,128)} %get-tuple-element.9), channel_id=1, source_target_pairs={{0,24},{8,0},{16,8},{24,16},{1,25},{9,1},{17,9},{25,17},{2,26},{10... | collective-permute-start | bytes 18440 | tf_op jit(solution)/shard_map/ppermute | solution.py:225
  49.5 1.4 %collective-permute-done.1 = f32[32,48]{1,0:T(8,128)S(1)} collective-permute-done((f32[32,48]{1,0:T(8,128)}, f32[32,48]{1,0:T(8,128)S(1)}, u32[]{:S(2)}, u32[]{:S(2)}) %collective-permute-start.1) | collective-permute-done | bytes 6176 | tf_op jit(solution)/shard_map/ppermute | solution.py:225
  50.9 0.9 %collective-permute-done.2 = f32[32,48]{1,0:T(8,128)S(1)} collective-permute-done((f32[32,48]{1,0:T(8,128)}, f32[32,48]{1,0:T(8,128)S(1)}, u32[]{:S(2)}, u32[]{:S(2)}) %collective-permute-start.2) | collective-permute-done | bytes 6176 | tf_op jit(solution)/shard_map/ppermute | solution.py:225
  51.8 0.7 add_add_fusion
  52.6 1.5 %collective-permute-start.4 = (f32[32,48]{1,0:T(8,128)S(1)}, f32[32,48]{1,0:T(8,128)S(1)}, u32[]{:S(2)}, u32[]{:S(2)}) collective-permute-start(f32[32,48]{1,0:T(8,128)S(1)} %add_add_fusion), channel_id=1, source_target_pairs={{0,4},{4,0},{1,5},{5,1},{2,6},{6,2},{3,7},{7,3},{8,12},{12,8},{9,1... | collective-permute-start | bytes 18440 | tf_op jit(solution)/shard_map/ppermute | solution.py:225
  54.1 2.3 %collective-permute-done.4 = f32[32,48]{1,0:T(8,128)S(1)} collective-permute-done((f32[32,48]{1,0:T(8,128)S(1)}, f32[32,48]{1,0:T(8,128)S(1)}, u32[]{:S(2)}, u32[]{:S(2)}) %collective-permute-start.4) | collective-permute-done | bytes 6176 | tf_op jit(solution)/shard_map/ppermute | solution.py:225
  56.4 1.8 %collective-permute-start.5 = (f32[32,48]{1,0:T(8,128)S(1)}, f32[32,48]{1,0:T(8,128)S(1)}, u32[]{:S(2)}, u32[]{:S(2)}) collective-permute-start(f32[32,48]{1,0:T(8,128)S(1)} %add.24), channel_id=1, source_target_pairs={{0,1},{1,2},{2,3},{3,0},{4,5},{5,6},{6,7},{7,4},{8,9},{9,10},{10,1... | collective-permute-start | bytes 18440 | tf_op jit(solution)/shard_map/ppermute | solution.py:225
  58.2 2.5 %collective-permute-start.6 = (f32[32,48]{1,0:T(8,128)S(1)}, f32[32,48]{1,0:T(8,128)S(1)}, u32[]{:S(2)}, u32[]{:S(2)}) collective-permute-start(f32[32,48]{1,0:T(8,128)S(1)} %add.24), channel_id=1, source_target_pairs={{0,2},{1,3},{2,0},{3,1},{4,6},{5,7},{6,4},{7,5},{8,10},{9,11},{10,... | collective-permute-start | bytes 18440 | tf_op jit(solution)/shard_map/ppermute | solution.py:225
  60.7 0.7 reshape.42.residual
  61.3 0.7 reshape.41.solution
  62.0 1.0 %collective-permute-done.6 = f32[32,48]{1,0:T(8,128)S(1)} collective-permute-done((f32[32,48]{1,0:T(8,128)S(1)}, f32[32,48]{1,0:T(8,128)S(1)}, u32[]{:S(2)}, u32[]{:S(2)}) %collective-permute-start.6) | collective-permute-done | bytes 6176 | tf_op jit(solution)/shard_map/ppermute | solution.py:225
  63.0 1.4 %collective-permute-done.7 = f32[32,48]{1,0:T(8,128)S(1)} collective-permute-done((f32[32,48]{1,0:T(8,128)S(1)}, f32[32,48]{1,0:T(8,128)S(1)}, u32[]{:S(2)}, u32[]{:S(2)}) %collective-permute-start.7) | collective-permute-done | bytes 6176 | tf_op jit(solution)/shard_map/ppermute | solution.py:225
  64.4 0.6 add_bitcast_fusion.grams
  65.0 5.7 %finish.1 = (f32[16,1024]{1,0:T(8,128)}, f32[16,1024]{1,0:T(8,128)}, f32[16,1024]{1,0:T(8,128)}) custom-call(f32[1,32,48]{2,1,0:T(8,128)} %add_bitcast_fusion.grams, f32[16,16]{1,0:T(8,128)} %gram_prev.1, f32[16,1024]{1,0:T(8,128)} %reshape.41.solution, f32[16,1024]{1,0:T(8,128)} %reshape.42.residual, f32[16,1024]{1,0:T(8,128)} %reshape.39.prev, ...), custom_call_target="tpu_custom_call" | custom-call | tf_op jit(solution)/shard_map/finish/pallas_call | solution.py:255
  70.7 1.5 %reshape.43 = f32[16,2,4,128]{3,2,1,0:T(4,128)} reshape(f32[16,1024]{1,0:T(8,128)} %get-tuple-element.12) | data formatting | bytes 131072 | tf_op jit(solution)/shard_map/reshape | solution.py:262
  72.3 0.7 reshape.44
  72.9 0.2 copy-done.4
  73.1 0.7 reshape.45
  (20 shorter events, 0.4 us)
Async XLA Ops:
  1.6 3.8 %copy-start.1 = (f32[16,2,4,128]{3,2,1,0:T(4,128)S(1)}, f32[16,2,4,128]{3,2,1,0:T(4,128)}, u32[]{:S(2)}) copy-start(f32[16,2,4,128]{3,2,1,0:T(4,128)} %param.7) | copy-start | bytes 196612
  1.7 5.3 %collective-permute-start = (f32[8,16,32]{2,1,0:T(8,128)S(1)}, f32[8,16,32]{2,1,0:T(8,128)S(1)}, u32[]{:S(2)}, u32[]{:S(2)}) collective-permute-start(f32[8,16,32]{2,1,0:T(8,128)S(1)} %pad_maximum_fusion.1), channel_id=1, source_target_pairs={{0,4},{4,0},{1,5},{5,1},{2,6},{6,2},{3,7},{7,3},{8,12},{12,8},{9,1... | collective-permute-start | bytes 49160 | tf_op jit(solution)/shard_map/ppermute | solution.py:42
  5.4 0.8 %copy-start.2 = (f32[16,2,4,128]{3,2,1,0:T(4,128)S(1)}, f32[16,2,4,128]{3,2,1,0:T(4,128)}, u32[]{:S(2)}) copy-start(f32[16,2,4,128]{3,2,1,0:T(4,128)} %param.8) | copy-start | bytes 196612
  47.5 13.2 %copy-start = (f32[16,2,4,128]{3,2,1,0:T(4,128)S(1)}, f32[16,2,4,128]{3,2,1,0:T(4,128)}, u32[]{:S(2)}) copy-start(f32[16,2,4,128]{3,2,1,0:T(4,128)} %param.6) | copy-start | bytes 196612
  47.5 3.4 %collective-permute-start.1 = (f32[32,48]{1,0:T(8,128)}, f32[32,48]{1,0:T(8,128)S(1)}, u32[]{:S(2)}, u32[]{:S(2)}) collective-permute-start(f32[32,48]{1,0:T(8,128)} %get-tuple-element.9), channel_id=1, source_target_pairs={{0,8},{8,16},{16,24},{24,0},{1,9},{9,17},{17,25},{25,1},{2,10},{10... | collective-permute-start | bytes 18440 | tf_op jit(solution)/shard_map/ppermute | solution.py:225
  47.9 3.9 %collective-permute-start.2 = (f32[32,48]{1,0:T(8,128)}, f32[32,48]{1,0:T(8,128)S(1)}, u32[]{:S(2)}, u32[]{:S(2)}) collective-permute-start(f32[32,48]{1,0:T(8,128)} %get-tuple-element.9), channel_id=1, source_target_pairs={{0,16},{8,24},{16,0},{24,8},{1,17},{9,25},{17,1},{25,9},{2,18},{10... | collective-permute-start | bytes 18440 | tf_op jit(solution)/shard_map/ppermute | solution.py:225
  48.4 3.4 %collective-permute-start.3 = (f32[32,48]{1,0:T(8,128)}, f32[32,48]{1,0:T(8,128)S(1)}, u32[]{:S(2)}, u32[]{:S(2)}) collective-permute-start(f32[32,48]{1,0:T(8,128)} %get-tuple-element.9), channel_id=1, source_target_pairs={{0,24},{8,0},{16,8},{24,16},{1,25},{9,1},{17,9},{25,17},{2,26},{10... | collective-permute-start | bytes 18440 | tf_op jit(solution)/shard_map/ppermute | solution.py:225
  52.6 3.9 %collective-permute-start.4 = (f32[32,48]{1,0:T(8,128)S(1)}, f32[32,48]{1,0:T(8,128)S(1)}, u32[]{:S(2)}, u32[]{:S(2)}) collective-permute-start(f32[32,48]{1,0:T(8,128)S(1)} %add_add_fusion), channel_id=1, source_target_pairs={{0,4},{4,0},{1,5},{5,1},{2,6},{6,2},{3,7},{7,3},{8,12},{12,8},{9,1... | collective-permute-start | bytes 18440 | tf_op jit(solution)/shard_map/ppermute | solution.py:225
  56.4 4.9 %copy-start.3 = (f32[16,2,4,128]{3,2,1,0:T(4,128)S(1)}, f32[16,2,4,128]{3,2,1,0:T(4,128)}, u32[]{:S(2)}) copy-start(f32[16,2,4,128]{3,2,1,0:T(4,128)} %param.5) | copy-start | bytes 196612
  56.4 5.6 %collective-permute-start.5 = (f32[32,48]{1,0:T(8,128)S(1)}, f32[32,48]{1,0:T(8,128)S(1)}, u32[]{:S(2)}, u32[]{:S(2)}) collective-permute-start(f32[32,48]{1,0:T(8,128)S(1)} %add.24), channel_id=1, source_target_pairs={{0,1},{1,2},{2,3},{3,0},{4,5},{5,6},{6,7},{7,4},{8,9},{9,10},{10,1... | collective-permute-start | bytes 18440 | tf_op jit(solution)/shard_map/ppermute | solution.py:225
  58.2 4.8 %collective-permute-start.6 = (f32[32,48]{1,0:T(8,128)S(1)}, f32[32,48]{1,0:T(8,128)S(1)}, u32[]{:S(2)}, u32[]{:S(2)}) collective-permute-start(f32[32,48]{1,0:T(8,128)S(1)} %add.24), channel_id=1, source_target_pairs={{0,2},{1,3},{2,0},{3,1},{4,6},{5,7},{6,4},{7,5},{8,10},{9,11},{10,... | collective-permute-start | bytes 18440 | tf_op jit(solution)/shard_map/ppermute | solution.py:225
  60.7 3.7 %collective-permute-start.7 = (f32[32,48]{1,0:T(8,128)S(1)}, f32[32,48]{1,0:T(8,128)S(1)}, u32[]{:S(2)}, u32[]{:S(2)}) collective-permute-start(f32[32,48]{1,0:T(8,128)S(1)} %add.24), channel_id=1, source_target_pairs={{0,3},{1,0},{2,1},{3,2},{4,7},{5,4},{6,5},{7,6},{8,11},{9,8},{10,9... | collective-permute-start | bytes 18440 | tf_op jit(solution)/shard_map/ppermute | solution.py:225
  70.7 1.5 %copy-start.5 = (f32[16,1024]{1,0:T(8,128)S(1)}, f32[16,1024]{1,0:T(8,128)}, u32[]{:S(2)}) copy-start(f32[16,1024]{1,0:T(8,128)} %get-tuple-element.13) | copy-start | bytes 196612
  72.3 0.8 %copy-start.4 = (f32[16,1024]{1,0:T(8,128)S(1)}, f32[16,1024]{1,0:T(8,128)}, u32[]{:S(2)}) copy-start(f32[16,1024]{1,0:T(8,128)} %get-tuple-element.14) | copy-start | bytes 196612

commit v2 on v1

--- a/solution.py
+++ b/solution.py
@@ -204,20 +204,31 @@
     return jnp.dot(left, right, precision=HIGHEST)
 
 
-def finish_kernel(grams, gram_prev, solution, residual, prev, image_prev, smoothed, image, solution_out, residual_out, direction_out):
-    n = gram_prev.shape[0]
+def invert_kernel(matrix, out):
+    order = matrix.shape[0]
+    row = lax.broadcasted_iota(jnp.int32, (order, order), 0)
+    col = lax.broadcasted_iota(jnp.int32, (order, order), 1)
+    out[...] = spd_solve(matrix[...], jnp.where(row == col, 1.0, 0.0).astype(jnp.float32))
+
+
+def finish_kernel(grams, inverse, solution, residual, prev, image_prev, smoothed, image, solution_out, residual_out, direction_out):
+    n = inverse.shape[0]
     total = jnp.sum(grams[...], axis=0)
     gram_zr, gram_zw, gram_zq = total[:n, :n], total[:n, n : 2 * n], total[:n, 2 * n :]
     gram_pw, gram_pq = total[n:, n : 2 * n], total[n:, 2 * n :]
-    beta = spd_solve(gram_prev[...], gram_zr)
+    beta = dot(inverse[...], gram_zr)
     turned = beta.T
     curvature = gram_zw + dot(gram_zq, beta) + dot(turned, gram_pw + dot(gram_pq, beta))
     direction = smoothed[...] + dot(turned, prev[...])
     image_new = image[...] + dot(turned, image_prev[...])
     alpha = spd_solve(curvature, gram_zr).T
-    direction_out[...] = direction
-    solution_out[...] = solution[...] + dot(alpha, direction)
-    residual_out[...] = residual[...] - dot(alpha, image_new)
+    values = (direction, solution[...] + dot(alpha, direction), residual[...] - dot(alpha, image_new))
+    _, lx, lz, lanes = direction_out.shape
+    for value, out in zip(values, (direction_out, solution_out, residual_out)):
+        for i in range(lx):
+            for j in range(lz):
+                at = (i * lz + j) * lanes
+                out[:, i, j, :] = value[:, at : at + lanes]
 
 
 def gather_grams(gram):
@@ -252,14 +263,21 @@
         name="smooth",
     )(where, upper, lower, flat[2], flat[3])
     grams = gather_grams(gram)
+    inverse = pl.pallas_call(
+        invert_kernel,
+        out_shape=jax.ShapeDtypeStruct(gram_prev.shape, jnp.float32),
+        in_specs=[vmem],
+        out_specs=vmem,
+        name="invert",
+    )(gram_prev)
     outs = pl.pallas_call(
         finish_kernel,
-        out_shape=(out, out, out),
+        out_shape=(jax.ShapeDtypeStruct(residual.shape, jnp.float32),) * 3,
         in_specs=[vmem] * 8,
         out_specs=(vmem,) * 3,
         name="finish",
-    )(grams, gram_prev, *flat, smoothed, image)
-    return tuple(v.reshape(residual.shape) for v in outs)
+    )(grams, inverse, *flat, smoothed, image)
+    return tuple(outs)
 
 
 def solution(mesh):

time: 74.2 us -> 70.1 us (0.945)
  local copies, waits for them, and re-layouts: 7.14 us -> 4.11 us
  waiting for transfers between devices: 7.17 us -> 4.78 us
  Pallas kernels: 14.2 us -> 15.7 us
    reshape x3 -> x0, local copies, waits for them, and re-layouts: 2.85 us -> none  [body(): return tuple((v.reshape(residual.shape) for v in outs))]
    ppermute x7, waiting for transfers between devices: 7.07 us -> 4.62 us  [gather_grams(): lax.ppermute(gram, axis, [(i, (i + k) % lax.axis_size(axis)) for i in ran...]
    pallas_call x1 -> x2, Pallas kernels: 5.7 us -> 7.16 us  [the longest x1 4.41 us: body(): pl.pallas_call(finish_kernel, out_shape=(jax.ShapeDtypeStruct(residual.sh...]
  transfers between devices with their start and end apart: 8 -> 8, of which waited for: 6 -> 4; matrix products, arithmetic and copies ran while one was open for 4% -> 5% of each run, Pallas kernels for 0% -> 4%
where the time goes in v2:
time: 70.1 us; the launch traced here: 69.7 us
  blocking collectives  31.6 us (45%)
  Pallas kernels  15.7 us (22%)
  starting transfers between devices  10.8 us (15%)
  waiting for transfers between devices  4.78 us (7%)
  local copies, waits for them, and re-layouts  4.11 us (6%)
  other arithmetic  2.02 us (3%)
    all_gather x3, blocking collectives, neighbours(): return lax.all_gather(value, axis)  31.6 us
    pallas_call x1, Pallas kernels, body(): pl.pallas_call(functools.partial(smooth_kernel, dims=(lx, lz, rows, lanes...  8.55 us
    ppermute x7, starting transfers between devices, gather_grams(): lax.ppermute(gram, axis, [(i, (i + k) % lax.axis_size(axis)) for i in ran...  7.74 us
    ppermute x7, waiting for transfers between devices, gather_grams(): lax.ppermute(gram, axis, [(i, (i + k) % lax.axis_size(axis)) for i in ran...  4.62 us
    pallas_call x1, Pallas kernels, body(): pl.pallas_call(finish_kernel, out_shape=(jax.ShapeDtypeStruct(residual.sh...  4.41 us
    ppermute x1, starting transfers between devices, beside(): lax.ppermute(jnp.concatenate([first, last], axis=-1), 'gy', [(0, 1), (1,...  3.06 us
    pallas_call x1, Pallas kernels, body(): pl.pallas_call(invert_kernel, out_shape=jax.ShapeDtypeStruct(gram_prev.sh...  2.75 us
    reshape x4, local copies, waits for them, and re-layouts, body(): v.reshape(rhs, rows * lanes)  2.6 us
  transfers between devices with their start and end apart: 8, of which 4 were waited for; matrix products, arithmetic and copies ran while one was open for 5% of the time, Pallas kernels for 4%

profile of v2, /device:TPU:0, one launch (start us, length us, event | category | flops | bytes accessed | tf_op | source)
XLA Modules:
  0.0 69.7 jit_solution(6471277252529369913)
XLA Ops:
  0.6 0.9 %copy.10 = f32[2,4,16,128]{3,2,1,0:T(8,128)S(1)} copy(f32[2,4,16,128]{3,1,0,2:T(4,128)} %bitcast.19) | data formatting | bytes 131072 | tf_op jit(solution)/shard_map/transpose | solution.py:248
  1.5 0.1 fusion.1
  1.6 0.1 pad_maximum_fusion.1
  1.7 3.1 %collective-permute-start = (f32[8,16,32]{2,1,0:T(8,128)S(1)}, f32[8,16,32]{2,1,0:T(8,128)S(1)}, u32[]{:S(2)}, u32[]{:S(2)}) collective-permute-start(f32[8,16,32]{2,1,0:T(8,128)S(1)} %pad_maximum_fusion.1), channel_id=1, source_target_pairs={{0,4},{4,0},{1,5},{5,1},{2,6},{6,2},{3,7},{7,3},{8,12},{12,8},{9,1... | collective-permute-start | bytes 49160 | tf_op jit(solution)/shard_map/ppermute | solution.py:42
  4.7 0.6 pad_add_fusion.where
  5.3 0.6 reshape.30.prev
  6.0 0.2 copy-done.2
  6.2 0.6 reshape.31.image_prev
  6.8 0.2 collective-permute-done
  7.0 0.1 reshape.28
  7.1 0.1 copy.13
  7.2 0.1 reshape.29
  7.3 14.8 %all-gather = f32[40,16,128]{2,1,0:T(8,128)S(1)} all-gather(f32[10,16,128]{2,1,0:T(8,128)S(1)} %pad_maximum_fusion), channel_id=2, replica_groups=mesh['gx'=4,'gy'=2,'gz'=4] {'gz'}, dimensions={0}, use_global_device_ids=true | all-gather | bytes 409600 | tf_op jit(solution)/shard_map/all_gather | solution.py:33
  22.2 8.3 %all-gather.1 = f32[16,10,8,128]{3,2,1,0:T(8,128)} all-gather(f32[4,10,8,128]{3,2,1,0:T(8,128)S(1)} %get-tuple-element.10), channel_id=3, replica_groups=mesh['gx'=4,'gy'=2,'gz'=4] {'gx'}, dimensions={0}, use_global_device_ids=true | all-gather | bytes 819200 | tf_op jit(solution)/shard_map/all_gather | solution.py:33
  30.5 8.4 %all-gather.2 = f32[16,10,8,128]{3,2,1,0:T(8,128)} all-gather(f32[4,10,8,128]{3,2,1,0:T(8,128)S(1)} %get-tuple-element.9), channel_id=4, replica_groups=mesh['gx'=4,'gy'=2,'gz'=4] {'gx'}, dimensions={0}, use_global_device_ids=true | all-gather | bytes 819200 | tf_op jit(solution)/shard_map/all_gather | solution.py:33
  38.9 8.6 %smooth.1 = (f32[16,1024]{1,0:T(8,128)}, f32[16,1024]{1,0:T(8,128)}, f32[32,48]{1,0:T(8,128)}) custom-call(s32[3]{0:T(128)} %pad_add_fusion.where, f32[4,4,10,8,128]{4,3,2,1,0:T(8,128)} %bitcast.13, f32[4,4,10,8,128]{4,3,2,1,0:T(8,128)} %bitcast.14, f32[16,1024]{1,0:T(8,128)} %reshape.30.prev, f32[16,1024]{1,0:T(8,128)} %reshape.31.image_prev), custom_call_target="tpu_custom_call" | custom-call | tf_op jit(solution)/shard_map/smooth/pallas_call | solution.py:257
  47.5 0.4 collective-permute-start.1
  47.8 0.5 collective-permute-start.2
  48.4 1.1 %collective-permute-start.3 = (f32[32,48]{1,0:T(8,128)}, f32[32,48]{1,0:T(8,128)S(1)}, u32[]{:S(2)}, u32[]{:S(2)}) collective-permute-start(f32[32,48]{1,0:T(8,128)} %get-tuple-element.6), channel_id=1, source_target_pairs={{0,24},{8,0},{16,8},{24,16},{1,25},{9,1},{17,9},{25,17},{2,26},{10... | collective-permute-start | bytes 18440 | tf_op jit(solution)/shard_map/ppermute | solution.py:236
  49.5 1.4 %collective-permute-done.1 = f32[32,48]{1,0:T(8,128)S(1)} collective-permute-done((f32[32,48]{1,0:T(8,128)}, f32[32,48]{1,0:T(8,128)S(1)}, u32[]{:S(2)}, u32[]{:S(2)}) %collective-permute-start.1) | collective-permute-done | bytes 6176 | tf_op jit(solution)/shard_map/ppermute | solution.py:236
  50.9 0.9 %collective-permute-done.2 = f32[32,48]{1,0:T(8,128)S(1)} collective-permute-done((f32[32,48]{1,0:T(8,128)}, f32[32,48]{1,0:T(8,128)S(1)}, u32[]{:S(2)}, u32[]{:S(2)}) %collective-permute-start.2) | collective-permute-done | bytes 6176 | tf_op jit(solution)/shard_map/ppermute | solution.py:236
  51.8 0.0 collective-permute-done.3
  51.8 0.7 %add_add_fusion = f32[32,48]{1,0:T(8,128)S(1)} fusion(f32[32,48]{1,0:T(8,128)S(1)} %collective-permute-done.3, f32[32,48]{1,0:T(8,128)S(1)} %collective-permute-done.2, f32[32,48]{1,0:T(8,128)} %get-tuple-element.6, f32[32,48]{1,0:T(8,128)S(1)} %collective-permute-done.1), kind=kLoop, calls=%fused_computation.4 | loop fusion | flops 4608 | bytes 30720 | tf_op jit(solution)/shard_map/add | solution.py:238
  52.5 1.6 %collective-permute-start.4 = (f32[32,48]{1,0:T(8,128)S(1)}, f32[32,48]{1,0:T(8,128)S(1)}, u32[]{:S(2)}, u32[]{:S(2)}) collective-permute-start(f32[32,48]{1,0:T(8,128)S(1)} %add_add_fusion), channel_id=1, source_target_pairs={{0,4},{4,0},{1,5},{5,1},{2,6},{6,2},{3,7},{7,3},{8,12},{12,8},{9,1... | collective-permute-start | bytes 18440 | tf_op jit(solution)/shard_map/ppermute | solution.py:236
  54.1 2.3 %collective-permute-done.4 = f32[32,48]{1,0:T(8,128)S(1)} collective-permute-done((f32[32,48]{1,0:T(8,128)S(1)}, f32[32,48]{1,0:T(8,128)S(1)}, u32[]{:S(2)}, u32[]{:S(2)}) %collective-permute-start.4) | collective-permute-done | bytes 6176 | tf_op jit(solution)/shard_map/ppermute | solution.py:236
  56.4 1.7 %collective-permute-start.5 = (f32[32,48]{1,0:T(8,128)S(1)}, f32[32,48]{1,0:T(8,128)S(1)}, u32[]{:S(2)}, u32[]{:S(2)}) collective-permute-start(f32[32,48]{1,0:T(8,128)S(1)} %add.24), channel_id=1, source_target_pairs={{0,1},{1,2},{2,3},{3,0},{4,5},{5,6},{6,7},{7,4},{8,9},{9,10},{10,1... | collective-permute-start | bytes 18440 | tf_op jit(solution)/shard_map/ppermute | solution.py:236
  58.1 2.5 %collective-permute-start.6 = (f32[32,48]{1,0:T(8,128)S(1)}, f32[32,48]{1,0:T(8,128)S(1)}, u32[]{:S(2)}, u32[]{:S(2)}) collective-permute-start(f32[32,48]{1,0:T(8,128)S(1)} %add.24), channel_id=1, source_target_pairs={{0,2},{1,3},{2,0},{3,1},{4,6},{5,7},{6,4},{7,5},{8,10},{9,11},{10,... | collective-permute-start | bytes 18440 | tf_op jit(solution)/shard_map/ppermute | solution.py:236
  60.6 0.7 reshape.33.residual
  61.2 0.6 reshape.32.solution
  61.9 2.8 %invert.1.inverse = f32[16,16]{1,0:T(8,128)} custom-call(f32[16,16]{1,0:T(8,128)} %matrix.1), custom_call_target="tpu_custom_call" | custom-call | tf_op jit(solution)/shard_map/invert/pallas_call | solution.py:266
  64.6 0.6 add_bitcast_fusion.grams
  65.3 4.4 %finish.1 = (f32[16,2,4,128]{3,2,1,0:T(4,128)}, f32[16,2,4,128]{3,2,1,0:T(4,128)}, f32[16,2,4,128]{3,2,1,0:T(4,128)}) custom-call(f32[1,32,48]{2,1,0:T(8,128)} %add_bitcast_fusion.grams, f32[16,16]{1,0:T(8,128)} %invert.1.inverse, f32[16,1024]{1,0:T(8,128)} %reshape.32.solution, f32[16,1024]{1,0:T(8,128)} %reshape.33.residual, f32[16,1024]{1,0:T(8,128)} %reshape.30.prev, ...), custom_call_target="tpu_custom_call" | custom-call | tf_op jit(solution)/shard_map/finish/pallas_call | solution.py:273
  (14 shorter events, 0.1 us)
Async XLA Ops:
  1.6 3.8 %copy-start.1 = (f32[16,2,4,128]{3,2,1,0:T(4,128)S(1)}, f32[16,2,4,128]{3,2,1,0:T(4,128)}, u32[]{:S(2)}) copy-start(f32[16,2,4,128]{3,2,1,0:T(4,128)} %param.7) | copy-start | bytes 196612
  1.7 5.3 %collective-permute-start = (f32[8,16,32]{2,1,0:T(8,128)S(1)}, f32[8,16,32]{2,1,0:T(8,128)S(1)}, u32[]{:S(2)}, u32[]{:S(2)}) collective-permute-start(f32[8,16,32]{2,1,0:T(8,128)S(1)} %pad_maximum_fusion.1), channel_id=1, source_target_pairs={{0,4},{4,0},{1,5},{5,1},{2,6},{6,2},{3,7},{7,3},{8,12},{12,8},{9,1... | collective-permute-start | bytes 49160 | tf_op jit(solution)/shard_map/ppermute | solution.py:42
  5.3 0.8 %copy-start.2 = (f32[16,2,4,128]{3,2,1,0:T(4,128)S(1)}, f32[16,2,4,128]{3,2,1,0:T(4,128)}, u32[]{:S(2)}) copy-start(f32[16,2,4,128]{3,2,1,0:T(4,128)} %param.8) | copy-start | bytes 196612
  47.5 13.1 %copy-start = (f32[16,2,4,128]{3,2,1,0:T(4,128)S(1)}, f32[16,2,4,128]{3,2,1,0:T(4,128)}, u32[]{:S(2)}) copy-start(f32[16,2,4,128]{3,2,1,0:T(4,128)} %param.6) | copy-start | bytes 196612
  47.5 3.4 %collective-permute-start.1 = (f32[32,48]{1,0:T(8,128)}, f32[32,48]{1,0:T(8,128)S(1)}, u32[]{:S(2)}, u32[]{:S(2)}) collective-permute-start(f32[32,48]{1,0:T(8,128)} %get-tuple-element.6), channel_id=1, source_target_pairs={{0,8},{8,16},{16,24},{24,0},{1,9},{9,17},{17,25},{25,1},{2,10},{10... | collective-permute-start | bytes 18440 | tf_op jit(solution)/shard_map/ppermute | solution.py:236
  47.8 3.9 %collective-permute-start.2 = (f32[32,48]{1,0:T(8,128)}, f32[32,48]{1,0:T(8,128)S(1)}, u32[]{:S(2)}, u32[]{:S(2)}) collective-permute-start(f32[32,48]{1,0:T(8,128)} %get-tuple-element.6), channel_id=1, source_target_pairs={{0,16},{8,24},{16,0},{24,8},{1,17},{9,25},{17,1},{25,9},{2,18},{10... | collective-permute-start | bytes 18440 | tf_op jit(solution)/shard_map/ppermute | solution.py:236
  48.4 3.4 %collective-permute-start.3 = (f32[32,48]{1,0:T(8,128)}, f32[32,48]{1,0:T(8,128)S(1)}, u32[]{:S(2)}, u32[]{:S(2)}) collective-permute-start(f32[32,48]{1,0:T(8,128)} %get-tuple-element.6), channel_id=1, source_target_pairs={{0,24},{8,0},{16,8},{24,16},{1,25},{9,1},{17,9},{25,17},{2,26},{10... | collective-permute-start | bytes 18440 | tf_op jit(solution)/shard_map/ppermute | solution.py:236
  52.5 3.9 %collective-permute-start.4 = (f32[32,48]{1,0:T(8,128)S(1)}, f32[32,48]{1,0:T(8,128)S(1)}, u32[]{:S(2)}, u32[]{:S(2)}) collective-permute-start(f32[32,48]{1,0:T(8,128)S(1)} %add_add_fusion), channel_id=1, source_target_pairs={{0,4},{4,0},{1,5},{5,1},{2,6},{6,2},{3,7},{7,3},{8,12},{12,8},{9,1... | collective-permute-start | bytes 18440 | tf_op jit(solution)/shard_map/ppermute | solution.py:236
  56.4 4.8 %copy-start.3 = (f32[16,2,4,128]{3,2,1,0:T(4,128)S(1)}, f32[16,2,4,128]{3,2,1,0:T(4,128)}, u32[]{:S(2)}) copy-start(f32[16,2,4,128]{3,2,1,0:T(4,128)} %param.5) | copy-start | bytes 196612
  56.4 8.2 %collective-permute-start.5 = (f32[32,48]{1,0:T(8,128)S(1)}, f32[32,48]{1,0:T(8,128)S(1)}, u32[]{:S(2)}, u32[]{:S(2)}) collective-permute-start(f32[32,48]{1,0:T(8,128)S(1)} %add.24), channel_id=1, source_target_pairs={{0,1},{1,2},{2,3},{3,0},{4,5},{5,6},{6,7},{7,4},{8,9},{9,10},{10,1... | collective-permute-start | bytes 18440 | tf_op jit(solution)/shard_map/ppermute | solution.py:236
  58.1 6.6 %collective-permute-start.6 = (f32[32,48]{1,0:T(8,128)S(1)}, f32[32,48]{1,0:T(8,128)S(1)}, u32[]{:S(2)}, u32[]{:S(2)}) collective-permute-start(f32[32,48]{1,0:T(8,128)S(1)} %add.24), channel_id=1, source_target_pairs={{0,2},{1,3},{2,0},{3,1},{4,6},{5,7},{6,4},{7,5},{8,10},{9,11},{10,... | collective-permute-start | bytes 18440 | tf_op jit(solution)/shard_map/ppermute | solution.py:236
  60.6 4.1 %collective-permute-start.7 = (f32[32,48]{1,0:T(8,128)S(1)}, f32[32,48]{1,0:T(8,128)S(1)}, u32[]{:S(2)}, u32[]{:S(2)}) collective-permute-start(f32[32,48]{1,0:T(8,128)S(1)} %add.24), channel_id=1, source_target_pairs={{0,3},{1,0},{2,1},{3,2},{4,7},{5,4},{6,5},{7,6},{8,11},{9,8},{10,9... | collective-permute-start | bytes 18440 | tf_op jit(solution)/shard_map/ppermute | solution.py:236

commit v3 on v2

--- a/solution.py
+++ b/solution.py
@@ -204,6 +204,11 @@
     return jnp.dot(left, right, precision=HIGHEST)
 
 
+def flattened(ref):
+    _, lx, lz, _ = ref.shape
+    return jnp.concatenate([ref[:, i, j, :] for i in range(lx) for j in range(lz)], axis=1)
+
+
 def invert_kernel(matrix, out):
     order = matrix.shape[0]
     row = lax.broadcasted_iota(jnp.int32, (order, order), 0)
@@ -222,7 +227,7 @@
     direction = smoothed[...] + dot(turned, prev[...])
     image_new = image[...] + dot(turned, image_prev[...])
     alpha = spd_solve(curvature, gram_zr).T
-    values = (direction, solution[...] + dot(alpha, direction), residual[...] - dot(alpha, image_new))
+    values = (direction, flattened(solution) + dot(alpha, direction), flattened(residual) - dot(alpha, image_new))
     _, lx, lz, lanes = direction_out.shape
     for value, out in zip(values, (direction_out, solution_out, residual_out)):
         for i in range(lx):
@@ -276,7 +281,7 @@
         in_specs=[vmem] * 8,
         out_specs=(vmem,) * 3,
         name="finish",
-    )(grams, inverse, *flat, smoothed, image)
+    )(grams, inverse, solution, residual, flat[2], flat[3], smoothed, image)
     return tuple(outs)
 
 

time: 70.1 us -> 69.7 us (level)
  local copies, waits for them, and re-layouts: 4.11 us -> 2.79 us
  waiting for transfers between devices: 4.78 us -> 5.74 us
    reshape x4 -> x2, local copies, waits for them, and re-layouts: 2.6 us -> 1.3 us  [body(): v.reshape(rhs, rows * lanes)]
    ppermute x7, waiting for transfers between devices: 4.62 us -> 5.6 us  [gather_grams(): lax.ppermute(gram, axis, [(i, (i + k) % lax.axis_size(axis)) for i in ran...]
  transfers between devices with their start and end apart: 8 -> 8, of which waited for: 4 -> 5; matrix products, arithmetic and copies ran while one was open for 5% -> 3% of each run, Pallas kernels for 4% -> 4%
where the time goes in v3:
time: 69.7 us; the launch traced here: 69.3 us
  blocking collectives  31.6 us (45%)
  Pallas kernels  15.7 us (23%)
  starting transfers between devices  10.8 us (15%)
  waiting for transfers between devices  5.74 us (8%)
  local copies, waits for them, and re-layouts  2.79 us (4%)
  other arithmetic  2.04 us (3%)
    all_gather x3, blocking collectives, neighbours(): return lax.all_gather(value, axis)  31.6 us
    pallas_call x1, Pallas kernels, body(): pl.pallas_call(functools.partial(smooth_kernel, dims=(lx, lz, rows, lanes...  8.55 us
    ppermute x7, starting transfers between devices, gather_grams(): lax.ppermute(gram, axis, [(i, (i + k) % lax.axis_size(axis)) for i in ran...  7.71 us
    ppermute x7, waiting for transfers between devices, gather_grams(): lax.ppermute(gram, axis, [(i, (i + k) % lax.axis_size(axis)) for i in ran...  5.6 us
    pallas_call x1, Pallas kernels, body(): pl.pallas_call(finish_kernel, out_shape=(jax.ShapeDtypeStruct(residual.sh...  4.42 us
    ppermute x1, starting transfers between devices, beside(): lax.ppermute(jnp.concatenate([first, last], axis=-1), 'gy', [(0, 1), (1,...  3.06 us
    pallas_call x1, Pallas kernels, body(): pl.pallas_call(invert_kernel, out_shape=jax.ShapeDtypeStruct(gram_prev.sh...  2.75 us
  transfers between devices with their start and end apart: 8, of which 5 were waited for; matrix products, arithmetic and copies ran while one was open for 3% of the time, Pallas kernels for 4%

profile of v3, /device:TPU:0, one launch (start us, length us, event | category | flops | bytes accessed | tf_op | source)
XLA Modules:
  0.0 69.3 jit_solution(14008405453746549889)
XLA Ops:
  0.6 0.9 %copy.10 = f32[2,4,16,128]{3,2,1,0:T(8,128)S(1)} copy(f32[2,4,16,128]{3,1,0,2:T(4,128)} %bitcast.19) | data formatting | bytes 131072 | tf_op jit(solution)/shard_map/transpose | solution.py:253
  1.5 0.1 fusion.1
  1.6 0.1 pad_maximum_fusion.1
  1.7 3.1 %collective-permute-start = (f32[8,16,32]{2,1,0:T(8,128)S(1)}, f32[8,16,32]{2,1,0:T(8,128)S(1)}, u32[]{:S(2)}, u32[]{:S(2)}) collective-permute-start(f32[8,16,32]{2,1,0:T(8,128)S(1)} %pad_maximum_fusion.1), channel_id=1, source_target_pairs={{0,4},{4,0},{1,5},{5,1},{2,6},{6,2},{3,7},{7,3},{8,12},{12,8},{9,1... | collective-permute-start | bytes 49160 | tf_op jit(solution)/shard_map/ppermute | solution.py:42
  4.7 0.6 pad_add_fusion.where
  5.4 0.7 reshape.24.prev
  6.0 0.2 copy-done.1
  6.2 0.7 reshape.25.image_prev
  6.8 0.1 collective-permute-done
  7.0 0.1 reshape.22
  7.1 0.1 copy.13
  7.2 0.1 reshape.23
  7.3 14.8 %all-gather = f32[40,16,128]{2,1,0:T(8,128)S(1)} all-gather(f32[10,16,128]{2,1,0:T(8,128)S(1)} %pad_maximum_fusion), channel_id=2, replica_groups=mesh['gx'=4,'gy'=2,'gz'=4] {'gz'}, dimensions={0}, use_global_device_ids=true | all-gather | bytes 409600 | tf_op jit(solution)/shard_map/all_gather | solution.py:33
  22.2 8.3 %all-gather.1 = f32[16,10,8,128]{3,2,1,0:T(8,128)} all-gather(f32[4,10,8,128]{3,2,1,0:T(8,128)S(1)} %get-tuple-element.10), channel_id=3, replica_groups=mesh['gx'=4,'gy'=2,'gz'=4] {'gx'}, dimensions={0}, use_global_device_ids=true | all-gather | bytes 819200 | tf_op jit(solution)/shard_map/all_gather | solution.py:33
  30.5 8.4 %all-gather.2 = f32[16,10,8,128]{3,2,1,0:T(8,128)} all-gather(f32[4,10,8,128]{3,2,1,0:T(8,128)S(1)} %get-tuple-element.9), channel_id=4, replica_groups=mesh['gx'=4,'gy'=2,'gz'=4] {'gx'}, dimensions={0}, use_global_device_ids=true | all-gather | bytes 819200 | tf_op jit(solution)/shard_map/all_gather | solution.py:33
  38.9 8.6 %smooth.1 = (f32[16,1024]{1,0:T(8,128)}, f32[16,1024]{1,0:T(8,128)}, f32[32,48]{1,0:T(8,128)}) custom-call(s32[3]{0:T(128)} %pad_add_fusion.where, f32[4,4,10,8,128]{4,3,2,1,0:T(8,128)} %bitcast.13, f32[4,4,10,8,128]{4,3,2,1,0:T(8,128)} %bitcast.14, f32[16,1024]{1,0:T(8,128)} %reshape.24.prev, f32[16,1024]{1,0:T(8,128)} %reshape.25.image_prev), custom_call_target="tpu_custom_call" | custom-call | tf_op jit(solution)/shard_map/smooth/pallas_call | solution.py:262
  47.5 0.4 collective-permute-start.1
  47.8 0.5 collective-permute-start.2
  48.4 1.1 %collective-permute-start.3 = (f32[32,48]{1,0:T(8,128)}, f32[32,48]{1,0:T(8,128)S(1)}, u32[]{:S(2)}, u32[]{:S(2)}) collective-permute-start(f32[32,48]{1,0:T(8,128)} %get-tuple-element.6), channel_id=1, source_target_pairs={{0,24},{8,0},{16,8},{24,16},{1,25},{9,1},{17,9},{25,17},{2,26},{10... | collective-permute-start | bytes 18440 | tf_op jit(solution)/shard_map/ppermute | solution.py:241
  49.5 1.4 %collective-permute-done.1 = f32[32,48]{1,0:T(8,128)S(1)} collective-permute-done((f32[32,48]{1,0:T(8,128)}, f32[32,48]{1,0:T(8,128)S(1)}, u32[]{:S(2)}, u32[]{:S(2)}) %collective-permute-start.1) | collective-permute-done | bytes 6176 | tf_op jit(solution)/shard_map/ppermute | solution.py:241
  50.9 0.9 %collective-permute-done.2 = f32[32,48]{1,0:T(8,128)S(1)} collective-permute-done((f32[32,48]{1,0:T(8,128)}, f32[32,48]{1,0:T(8,128)S(1)}, u32[]{:S(2)}, u32[]{:S(2)}) %collective-permute-start.2) | collective-permute-done | bytes 6176 | tf_op jit(solution)/shard_map/ppermute | solution.py:241
  51.8 0.7 %add_add_fusion = f32[32,48]{1,0:T(8,128)S(1)} fusion(f32[32,48]{1,0:T(8,128)S(1)} %collective-permute-done.3, f32[32,48]{1,0:T(8,128)S(1)} %collective-permute-done.2, f32[32,48]{1,0:T(8,128)} %get-tuple-element.6, f32[32,48]{1,0:T(8,128)S(1)} %collective-permute-done.1), kind=kLoop, calls=%fused_computation.4 | loop fusion | flops 4608 | bytes 30720 | tf_op jit(solution)/shard_map/add | solution.py:243
  52.5 1.6 %collective-permute-start.4 = (f32[32,48]{1,0:T(8,128)S(1)}, f32[32,48]{1,0:T(8,128)S(1)}, u32[]{:S(2)}, u32[]{:S(2)}) collective-permute-start(f32[32,48]{1,0:T(8,128)S(1)} %add_add_fusion), channel_id=1, source_target_pairs={{0,4},{4,0},{1,5},{5,1},{2,6},{6,2},{3,7},{7,3},{8,12},{12,8},{9,1... | collective-permute-start | bytes 18440 | tf_op jit(solution)/shard_map/ppermute | solution.py:241
  54.1 2.3 %collective-permute-done.4 = f32[32,48]{1,0:T(8,128)S(1)} collective-permute-done((f32[32,48]{1,0:T(8,128)S(1)}, f32[32,48]{1,0:T(8,128)S(1)}, u32[]{:S(2)}, u32[]{:S(2)}) %collective-permute-start.4) | collective-permute-done | bytes 6176 | tf_op jit(solution)/shard_map/ppermute | solution.py:241
  56.4 1.7 %collective-permute-start.5 = (f32[32,48]{1,0:T(8,128)S(1)}, f32[32,48]{1,0:T(8,128)S(1)}, u32[]{:S(2)}, u32[]{:S(2)}) collective-permute-start(f32[32,48]{1,0:T(8,128)S(1)} %add.24), channel_id=1, source_target_pairs={{0,1},{1,2},{2,3},{3,0},{4,5},{5,6},{6,7},{7,4},{8,9},{9,10},{10,1... | collective-permute-start | bytes 18440 | tf_op jit(solution)/shard_map/ppermute | solution.py:241
  58.1 2.5 %collective-permute-start.6 = (f32[32,48]{1,0:T(8,128)S(1)}, f32[32,48]{1,0:T(8,128)S(1)}, u32[]{:S(2)}, u32[]{:S(2)}) collective-permute-start(f32[32,48]{1,0:T(8,128)S(1)} %add.24), channel_id=1, source_target_pairs={{0,2},{1,3},{2,0},{3,1},{4,6},{5,7},{6,4},{7,5},{8,10},{9,11},{10,... | collective-permute-start | bytes 18440 | tf_op jit(solution)/shard_map/ppermute | solution.py:241
  60.6 2.8 %invert.1.inverse = f32[16,16]{1,0:T(8,128)} custom-call(f32[16,16]{1,0:T(8,128)} %matrix.1), custom_call_target="tpu_custom_call" | custom-call | tf_op jit(solution)/shard_map/invert/pallas_call | solution.py:271
  63.3 0.0 collective-permute-done.5
  63.3 0.0 collective-permute-done.6
  63.3 1.0 %collective-permute-done.7 = f32[32,48]{1,0:T(8,128)S(1)} collective-permute-done((f32[32,48]{1,0:T(8,128)S(1)}, f32[32,48]{1,0:T(8,128)S(1)}, u32[]{:S(2)}, u32[]{:S(2)}) %collective-permute-start.7) | collective-permute-done | bytes 6176 | tf_op jit(solution)/shard_map/ppermute | solution.py:241
  64.3 0.6 add_bitcast_fusion.grams
  64.9 4.4 %finish.1 = (f32[16,2,4,128]{3,2,1,0:T(4,128)}, f32[16,2,4,128]{3,2,1,0:T(4,128)}, f32[16,2,4,128]{3,2,1,0:T(4,128)}) custom-call(f32[1,32,48]{2,1,0:T(8,128)} %add_bitcast_fusion.grams, f32[16,16]{1,0:T(8,128)} %invert.1.inverse, f32[16,2,4,128]{3,2,1,0:T(4,128)} %solution.1, f32[16,2,4,128]{3,2,1,0:T(4,128)} %residual.1, f32[16,1024]{1,0:T(8,128)} %reshape.24.prev, ...), custom_call_target="tpu_custom_call" | custom-call | tf_op jit(solution)/shard_map/finish/pallas_call | solution.py:278
  (8 shorter events, 0.0 us)
Async XLA Ops:
  1.6 3.8 %copy-start = (f32[16,2,4,128]{3,2,1,0:T(4,128)S(1)}, f32[16,2,4,128]{3,2,1,0:T(4,128)}, u32[]{:S(2)}) copy-start(f32[16,2,4,128]{3,2,1,0:T(4,128)} %param.7) | copy-start | bytes 196612
  1.7 5.3 %collective-permute-start = (f32[8,16,32]{2,1,0:T(8,128)S(1)}, f32[8,16,32]{2,1,0:T(8,128)S(1)}, u32[]{:S(2)}, u32[]{:S(2)}) collective-permute-start(f32[8,16,32]{2,1,0:T(8,128)S(1)} %pad_maximum_fusion.1), channel_id=1, source_target_pairs={{0,4},{4,0},{1,5},{5,1},{2,6},{6,2},{3,7},{7,3},{8,12},{12,8},{9,1... | collective-permute-start | bytes 49160 | tf_op jit(solution)/shard_map/ppermute | solution.py:42
  5.4 0.8 %copy-start.1 = (f32[16,2,4,128]{3,2,1,0:T(4,128)S(1)}, f32[16,2,4,128]{3,2,1,0:T(4,128)}, u32[]{:S(2)}) copy-start(f32[16,2,4,128]{3,2,1,0:T(4,128)} %param.8) | copy-start | bytes 196612
  47.5 3.4 %collective-permute-start.1 = (f32[32,48]{1,0:T(8,128)}, f32[32,48]{1,0:T(8,128)S(1)}, u32[]{:S(2)}, u32[]{:S(2)}) collective-permute-start(f32[32,48]{1,0:T(8,128)} %get-tuple-element.6), channel_id=1, source_target_pairs={{0,8},{8,16},{16,24},{24,0},{1,9},{9,17},{17,25},{25,1},{2,10},{10... | collective-permute-start | bytes 18440 | tf_op jit(solution)/shard_map/ppermute | solution.py:241
  47.8 3.9 %collective-permute-start.2 = (f32[32,48]{1,0:T(8,128)}, f32[32,48]{1,0:T(8,128)S(1)}, u32[]{:S(2)}, u32[]{:S(2)}) collective-permute-start(f32[32,48]{1,0:T(8,128)} %get-tuple-element.6), channel_id=1, source_target_pairs={{0,16},{8,24},{16,0},{24,8},{1,17},{9,25},{17,1},{25,9},{2,18},{10... | collective-permute-start | bytes 18440 | tf_op jit(solution)/shard_map/ppermute | solution.py:241
  48.4 3.4 %collective-permute-start.3 = (f32[32,48]{1,0:T(8,128)}, f32[32,48]{1,0:T(8,128)S(1)}, u32[]{:S(2)}, u32[]{:S(2)}) collective-permute-start(f32[32,48]{1,0:T(8,128)} %get-tuple-element.6), channel_id=1, source_target_pairs={{0,24},{8,0},{16,8},{24,16},{1,25},{9,1},{17,9},{25,17},{2,26},{10... | collective-permute-start | bytes 18440 | tf_op jit(solution)/shard_map/ppermute | solution.py:241
  52.5 3.9 %collective-permute-start.4 = (f32[32,48]{1,0:T(8,128)S(1)}, f32[32,48]{1,0:T(8,128)S(1)}, u32[]{:S(2)}, u32[]{:S(2)}) collective-permute-start(f32[32,48]{1,0:T(8,128)S(1)} %add_add_fusion), channel_id=1, source_target_pairs={{0,4},{4,0},{1,5},{5,1},{2,6},{6,2},{3,7},{7,3},{8,12},{12,8},{9,1... | collective-permute-start | bytes 18440 | tf_op jit(solution)/shard_map/ppermute | solution.py:241
  56.4 6.9 %collective-permute-start.5 = (f32[32,48]{1,0:T(8,128)S(1)}, f32[32,48]{1,0:T(8,128)S(1)}, u32[]{:S(2)}, u32[]{:S(2)}) collective-permute-start(f32[32,48]{1,0:T(8,128)S(1)} %add.24), channel_id=1, source_target_pairs={{0,1},{1,2},{2,3},{3,0},{4,5},{5,6},{6,7},{7,4},{8,9},{9,10},{10,1... | collective-permute-start | bytes 18440 | tf_op jit(solution)/shard_map/ppermute | solution.py:241
  58.1 5.2 %collective-permute-start.6 = (f32[32,48]{1,0:T(8,128)S(1)}, f32[32,48]{1,0:T(8,128)S(1)}, u32[]{:S(2)}, u32[]{:S(2)}) collective-permute-start(f32[32,48]{1,0:T(8,128)S(1)} %add.24), channel_id=1, source_target_pairs={{0,2},{1,3},{2,0},{3,1},{4,6},{5,7},{6,4},{7,5},{8,10},{9,11},{10,... | collective-permute-start | bytes 18440 | tf_op jit(solution)/shard_map/ppermute | solution.py:241
  60.6 3.7 %collective-permute-start.7 = (f32[32,48]{1,0:T(8,128)S(1)}, f32[32,48]{1,0:T(8,128)S(1)}, u32[]{:S(2)}, u32[]{:S(2)}) collective-permute-start(f32[32,48]{1,0:T(8,128)S(1)} %add.24), channel_id=1, source_target_pairs={{0,3},{1,0},{2,1},{3,2},{4,7},{5,4},{6,5},{7,6},{8,11},{9,8},{10,9... | collective-permute-start | bytes 18440 | tf_op jit(solution)/shard_map/ppermute | solution.py:241
